TPU v7x, 256 devices: a whole 4x4x8 slice. The times are simulated.
256 devices in a mesh: mem: 8 (over x_lo, y), tile: 32 (over z, x_hi, core).
Axes of the slice: x: 4 (x_hi: 2, x_lo: 2; x = x_hi * 2 + x_lo), y: 4, z: 8, core: 2. Of those that a mesh axis runs over, the one named last changes fastest.
Arguments:
- perturbations: bfloat16 [3, 256, 512, 256], P(None, 'mem', 'tile'), may hold values from -0.375 to 0.375
- control: float32 [256, 512, 256], P('mem', 'tile'), may hold values from -15 to 15
- innovation: float32 [3, 512, 256], P(None, 'tile'), may hold values from -6 to 6
- obs_weight: float32 [3, 512, 256], P(None, 'tile'), may hold values from 2 to 32
- diffusion: float32 [512, 256], P('tile'), may hold values from 0.04 to 0.18
- advection: float32 [512, 256], P('tile'), may hold values from 0.08 to 0.3
- upwind: int32 [512, 256], P('tile'), may hold values from 0 to 1
Outputs:
- gradient: float32 [256, 512, 256], P('mem', 'tile')
- hessian_product: float32 [256, 512, 256], P('mem', 'tile')
- step_length: float32 [], replicated
All inputs are finite; a program needn't handle non-finite values.
Results may differ from a plain program's by a relative error of at most 0.0003.
Values sent between devices are 32-bit elements; how exact they have to be, the bound alone decides.
A program may use at most 64 MiB of HBM per device.

v0:
```python
import functools

import jax
import jax.numpy as jnp
from jax import lax
from jax.sharding import Mesh
from jax.sharding import PartitionSpec as P

SWEEPS = 4
TILE = ("tile_0", "tile_1", "tile_2")
MEM = ("mem_0", "mem_1")
MEM_TILE = ("mem_0", "mem_1", "tile_0", "tile_1", "tile_2")


def extended_2(block, sides, width):
    for axis, dim in sides:
        count = lax.axis_size(axis)
        forward = [(i, i + 1) for i in range(count - 1)]
        backward = [(target, source) for source, target in forward]
        low = lax.ppermute(
            lax.slice_in_dim(block, block.shape[dim] - width, None, axis=dim), axis, forward
        )
        high = lax.ppermute(lax.slice_in_dim(block, 0, width, axis=dim), axis, backward)
        block = jnp.concatenate([low, block, high], axis=dim)
    return block


def sent_to_all(x, axis):
    devices = lax.axis_size(axis)
    return lax.all_to_all(jnp.broadcast_to(x[None], (devices, *x.shape)), axis, 0, 0, tiled=True)


def of_everyone(x, axis):
    everything = sent_to_all(x, axis)
    return jnp.sum(everything, axis=0)


def over_axes(x, axes):
    return functools.reduce(lax.psum, axes, x)


def column_pad(values):
    return jnp.pad(values, ((0, 0), (0, 0), (1, 1)))


def forward_core(extended, kappa_rows, advect_rows, upper_rows):
    center = extended[:, 1:-1]
    below = extended[:, 2:]
    above = extended[:, :-2]
    padded = column_pad(center)
    spread = below + above + padded[:, :, 2:] + padded[:, :, :-2] - 4.0 * center
    upwind_value = jnp.where(upper_rows, below, above)
    return center + kappa_rows * spread - advect_rows * (center - upwind_value)


def adjoint_core(center, carried, weighted_ext, lower_ext, upper_ext):
    weighted = weighted_ext[:, 1:-1]
    padded = column_pad(weighted)
    spread = (
        weighted_ext[:, 2:]
        + weighted_ext[:, :-2]
        + padded[:, :, 2:]
        + padded[:, :, :-2]
        - 4.0 * weighted
    )
    returned = lower_ext[:, 2:] + upper_ext[:, :-2]
    return center + spread - carried + returned


def shards(perturbations, control, innovation, obs_weight, diffusion, advection, upwind):
    row_count = control.shape[1]
    upper = upwind == 1
    stacked_coeff = jnp.stack([diffusion, advection, upper.astype(jnp.float32)])
    coefficients = extended_2(stacked_coeff, ((TILE, 1),), SWEEPS)
    kappa_wide = coefficients[0]
    advect_wide = coefficients[1]
    upper_wide = coefficients[2] > 0.5
    global_rows = (
        lax.axis_index(TILE) * row_count
        + jnp.arange(row_count + 2 * SWEEPS, dtype=jnp.int32)
        - SWEEPS
    )
    inside = ((global_rows >= 0) & (global_rows < row_count * lax.axis_size(TILE))).astype(
        jnp.float32
    )[:, None]

    def localise(values):
        extended = extended_2(values, ((TILE, 1),), SWEEPS)
        for repeat in range(SWEEPS):
            first_row = repeat + 1
            last_row = row_count + 2 * SWEEPS - repeat - 1
            extended = (
                forward_core(
                    extended,
                    kappa_wide[first_row:last_row],
                    advect_wide[first_row:last_row],
                    upper_wide[first_row:last_row],
                )
                * inside[first_row:last_row]
            )
        return extended

    def localise_adjoint(values):
        extended = extended_2(values, ((TILE, 1),), SWEEPS)
        for repeat in range(SWEEPS):
            last_row = row_count + 2 * SWEEPS - repeat
            upper_part = upper_wide[repeat:last_row]
            carried = advect_wide[repeat:last_row] * extended
            weighted = kappa_wide[repeat:last_row] * extended
            lower_ext = jnp.where(upper_part, 0.0, carried)
            upper_ext = jnp.where(upper_part, carried, 0.0)
            extended = (
                adjoint_core(extended[:, 1:-1], carried[:, 1:-1], weighted, lower_ext, upper_ext)
                * inside[repeat + 1 : last_row - 1]
            )
        return extended

    def project(values):
        return jnp.sum(perturbations.astype(jnp.float32) * values[None], axis=1)

    def pull_back(weights_time):
        return jnp.sum(perturbations.astype(jnp.float32) * weights_time[:, None], axis=0)

    def misfit_of(partial_value, subtract):
        total = of_everyone(partial_value, MEM)
        if subtract:
            whole_misfit = obs_weight * (total - innovation)
        else:
            whole_misfit = obs_weight * total
        local_term = jnp.where(lax.axis_index(MEM) == 0, jnp.sum(total * whole_misfit), 0.0)
        return (whole_misfit, local_term)

    misfit, unused_term = misfit_of(project(localise(control)), True)
    gradient = control + localise_adjoint(pull_back(misfit))
    weighted_image, curvature_term = misfit_of(project(localise(gradient)), False)
    hessian_product = gradient + localise_adjoint(pull_back(weighted_image))
    squares, obs_total = (
        over_axes(jnp.sum(gradient * gradient), MEM_TILE),
        over_axes(curvature_term, MEM_TILE),
    )
    return (gradient, hessian_product, squares / (squares + obs_total))


def solution(mesh):
    finer = Mesh(
        mesh.devices.reshape(2, 4, 8, 2, 2), ("mem_0", "mem_1", "tile_0", "tile_1", "tile_2")
    )
    placed = (
        P(None, MEM, TILE, None),
        P(MEM, TILE, None),
        P(None, TILE, None),
        P(None, TILE, None),
        P(TILE, None),
        P(TILE, None),
        P(TILE, None),
    )
    return jax.shard_map(
        shards,
        mesh=finer,
        in_specs=placed,
        out_specs=(P(MEM, TILE, None), P(MEM, TILE, None), P()),
        check_vma=False,
    )
```

profile of v0, /device:TPU:1, one launch (start us, length us, event | category | flops | bytes accessed | tf_op | source)
XLA Modules:
  0.0 146.3 jit_solution(11762765304300313483)
XLA Ops:
  0.6 0.8 convert_bitcast_fusion
  1.4 0.8 pad_maximum_fusion.7
  2.2 6.0 %collective-permute-start.2 = (f32[3,4,256]{2,1,0:T(4,128)S(1)}, f32[3,4,256]{2,1,0:T(4,128)S(1)}, u32[]{:S(2)}, u32[]{:S(2)}) collective-permute-start(f32[3,4,256]{2,1,0:T(4,128)S(1)} %get-tuple-element.51), channel_id=1, source_target_pairs={{0,1},{1,2},{2,3},{3,4},{4,5},{5,6},{6,7},{7,8},{8,9},{9,10},{10,1... | collective-permute-start | bytes 36872 | tf_op jit(solution)/shard_map/ppermute | solution.py:20
  8.2 1.9 %collective-permute-start.3 = (f32[3,4,256]{2,1,0:T(4,128)S(1)}, f32[3,4,256]{2,1,0:T(4,128)S(1)}, u32[]{:S(2)}, u32[]{:S(2)}) collective-permute-start(f32[3,4,256]{2,1,0:T(4,128)S(1)} %get-tuple-element.52), channel_id=1, source_target_pairs={{1,0},{2,1},{3,2},{4,3},{5,4},{6,5},{7,6},{8,7},{9,8},{10,9},{11,1... | collective-permute-start | bytes 36872 | tf_op jit(solution)/shard_map/ppermute | solution.py:23
  10.1 1.1 fusion.136
  11.2 5.1 %collective-permute-start = (f32[32,4,256]{2,1,0:T(4,128)S(1)}, f32[32,4,256]{2,1,0:T(4,128)S(1)}, u32[]{:S(2)}, u32[]{:S(2)}) collective-permute-start(f32[32,4,256]{2,1,0:T(4,128)S(1)} %get-tuple-element.41), channel_id=1, source_target_pairs={{0,1},{1,2},{2,3},{3,4},{4,5},{5,6},{6,7},{7,8},{8,9},{9,10},{10,1... | collective-permute-start | bytes 393224 | tf_op jit(solution)/shard_map/ppermute | solution.py:20
  16.4 1.9 %collective-permute-start.1 = (f32[32,4,256]{2,1,0:T(4,128)S(1)}, f32[32,4,256]{2,1,0:T(4,128)S(1)}, u32[]{:S(2)}, u32[]{:S(2)}) collective-permute-start(f32[32,4,256]{2,1,0:T(4,128)S(1)} %get-tuple-element.42), channel_id=1, source_target_pairs={{1,0},{2,1},{3,2},{4,3},{5,4},{6,5},{7,6},{8,7},{9,8},{10,9},{11,1... | collective-permute-start | bytes 393224 | tf_op jit(solution)/shard_map/ppermute | solution.py:23
  18.6 0.8 pad_maximum_fusion.4
  19.6 4.6 %collective-permute-done.1 = f32[32,4,256]{2,1,0:T(4,128)S(1)} collective-permute-done((f32[32,4,256]{2,1,0:T(4,128)S(1)}, f32[32,4,256]{2,1,0:T(4,128)S(1)}, u32[]{:S(2)}, u32[]{:S(2)}) %collective-permute-start.1) | collective-permute-done | bytes 131104 | tf_op jit(solution)/shard_map/ppermute | solution.py:23
  24.4 0.7 fusion.10
  25.1 0.7 fusion.17
  25.9 0.7 fusion.24
  26.7 0.6 copy-done.3
  27.4 0.5 fusion.100
  27.8 0.7 copy-done
  28.7 0.8 broadcast_in_dim.86
  29.5 4.4 %all-to-all-start = ((f32[8,3,16,256]{3,2,1,0:T(8,128)}), f32[8,3,16,256]{3,2,1,0:T(8,128)S(1)}, u32[]{:S(2)}, u32[]{:S(2)}) async-start(f32[8,3,16,256]{3,2,1,0:T(8,128)} %broadcast_in_dim.86), calls=%async_computation | async-start | bytes 786432 | tf_op jit(solution)/shard_map/all_to_all | solution.py:30
  33.8 6.6 %all-to-all-done = f32[8,3,16,256]{3,2,1,0:T(8,128)S(1)} async-done(((f32[8,3,16,256]{3,2,1,0:T(8,128)}), f32[8,3,16,256]{3,2,1,0:T(8,128)S(1)}, u32[]{:S(2)}, u32[]{:S(2)}) %all-to-all-start) | async-done | bytes 393248 | tf_op jit(solution)/shard_map/all_to_all | solution.py:30
  40.7 3.8 %collective-permute-start.4 = (f32[32,4,256]{2,1,0:T(4,128)S(1)}, f32[32,4,256]{2,1,0:T(4,128)S(1)}, u32[]{:S(2)}, u32[]{:S(2)}) collective-permute-start(f32[32,4,256]{2,1,0:T(4,128)S(1)} %get-tuple-element.39), channel_id=1, source_target_pairs={{0,1},{1,2},{2,3},{3,4},{4,5},{5,6},{6,7},{7,8},{8,9},{9,10},{10,1... | collective-permute-start | bytes 393224 | tf_op jit(solution)/shard_map/ppermute | solution.py:20
  44.5 1.9 %collective-permute-start.5 = (f32[32,4,256]{2,1,0:T(4,128)S(1)}, f32[32,4,256]{2,1,0:T(4,128)S(1)}, u32[]{:S(2)}, u32[]{:S(2)}) collective-permute-start(f32[32,4,256]{2,1,0:T(4,128)S(1)} %get-tuple-element.40), channel_id=1, source_target_pairs={{1,0},{2,1},{3,2},{4,3},{5,4},{6,5},{7,6},{8,7},{9,8},{10,9},{11,1... | collective-permute-start | bytes 393224 | tf_op jit(solution)/shard_map/ppermute | solution.py:23
  46.5 6.0 %collective-permute-done.5 = f32[32,4,256]{2,1,0:T(4,128)S(1)} collective-permute-done((f32[32,4,256]{2,1,0:T(4,128)S(1)}, f32[32,4,256]{2,1,0:T(4,128)S(1)}, u32[]{:S(2)}, u32[]{:S(2)}) %collective-permute-start.5) | collective-permute-done | bytes 131104 | tf_op jit(solution)/shard_map/ppermute | solution.py:23
  52.5 0.2 pad_maximum_fusion.1
  52.7 0.7 broadcast_multiply_fusion.13
  53.6 0.7 broadcast_multiply_fusion.9
  54.4 0.7 broadcast_multiply_fusion.5
  55.3 1.2 multiply_reduce_fusion
  56.5 2.0 %collective-permute-start.6 = (f32[32,4,256]{2,1,0:T(4,128)S(1)}, f32[32,4,256]{2,1,0:T(4,128)S(1)}, u32[]{:S(2)}, u32[]{:S(2)}) collective-permute-start(f32[32,4,256]{2,1,0:T(4,128)S(1)} %get-tuple-element.37), channel_id=1, source_target_pairs={{0,1},{1,2},{2,3},{3,4},{4,5},{5,6},{6,7},{7,8},{8,9},{9,10},{10,1... | collective-permute-start | bytes 393224 | tf_op jit(solution)/shard_map/ppermute | solution.py:20
  58.5 2.4 %collective-permute-start.7 = (f32[32,4,256]{2,1,0:T(4,128)S(1)}, f32[32,4,256]{2,1,0:T(4,128)S(1)}, u32[]{:S(2)}, u32[]{:S(2)}) collective-permute-start(f32[32,4,256]{2,1,0:T(4,128)S(1)} %get-tuple-element.38), channel_id=1, source_target_pairs={{1,0},{2,1},{3,2},{4,3},{5,4},{6,5},{7,6},{8,7},{9,8},{10,9},{11,1... | collective-permute-start | bytes 393224 | tf_op jit(solution)/shard_map/ppermute | solution.py:23
  60.9 8.1 %collective-permute-done.7 = f32[32,4,256]{2,1,0:T(4,128)S(1)} collective-permute-done((f32[32,4,256]{2,1,0:T(4,128)S(1)}, f32[32,4,256]{2,1,0:T(4,128)S(1)}, u32[]{:S(2)}, u32[]{:S(2)}) %collective-permute-start.7) | collective-permute-done | bytes 131104 | tf_op jit(solution)/shard_map/ppermute | solution.py:23
  69.2 0.7 fusion.52
  70.0 0.7 fusion.59
  70.7 0.7 fusion.66
  71.5 0.5 fusion.115
  71.9 0.2 fusion.2
  72.2 9.6 %all_to_all.10 = f32[8,3,16,256]{3,2,1,0:T(8,128)S(1)} all-to-all(f32[8,3,16,256]{3,2,1,0:T(8,128)S(1)} %broadcast_in_dim.92), channel_id=1, replica_groups=mesh['mem_0'=2,'mem_1'=4,'tile_0'=8,'tile_1'=2,'tile_2'=2] {'mem_0','mem..., dimensions={0} | all-to-all | bytes 786432 | tf_op jit(solution)/shard_map/all_to_all | solution.py:30
  81.8 0.6 multiply_reduce_fusion.1
  82.6 3.8 %collective-permute-start.8 = (f32[32,4,256]{2,1,0:T(4,128)S(1)}, f32[32,4,256]{2,1,0:T(4,128)S(1)}, u32[]{:S(2)}, u32[]{:S(2)}) collective-permute-start(f32[32,4,256]{2,1,0:T(4,128)S(1)} %get-tuple-element.35), channel_id=1, source_target_pairs={{0,1},{1,2},{2,3},{3,4},{4,5},{5,6},{6,7},{7,8},{8,9},{9,10},{10,1... | collective-permute-start | bytes 393224 | tf_op jit(solution)/shard_map/ppermute | solution.py:20
  86.4 1.9 %collective-permute-start.9 = (f32[32,4,256]{2,1,0:T(4,128)S(1)}, f32[32,4,256]{2,1,0:T(4,128)S(1)}, u32[]{:S(2)}, u32[]{:S(2)}) collective-permute-start(f32[32,4,256]{2,1,0:T(4,128)S(1)} %get-tuple-element.36), channel_id=1, source_target_pairs={{1,0},{2,1},{3,2},{4,3},{5,4},{6,5},{7,6},{8,7},{9,8},{10,9},{11,1... | collective-permute-start | bytes 393224 | tf_op jit(solution)/shard_map/ppermute | solution.py:23
  89.0 4.4 %all-reduce.20 = (f32[]{:T(128)}, f32[]{:T(128)}) all-reduce(f32[]{:T(128)} %get-tuple-element.15, f32[]{:T(128)S(6)} %select_n.112), channel_id=1, replica_groups=mesh['mem_0'=2,'mem_1'=4,'tile_0'=8,'tile_1'=2,'tile_2'=2] {'mem_0'}, use_global_device_ids=true, to_apply=%region_7.8 | all-reduce | flops 2 | bytes 16 | tf_op jit(solution)/shard_map/psum | solution.py:39
  93.4 7.4 %all-reduce.17 = (f32[]{:T(128)}, f32[]{:T(128)}) all-reduce(f32[]{:T(128)} %get-tuple-element.11, f32[]{:T(128)} %get-tuple-element.12), channel_id=1, replica_groups=mesh['mem_0'=2,'mem_1'=4,'tile_0'=8,'tile_1'=2,'tile_2'=2] {'mem_1'}, use_global_device_ids=true, to_apply=%region_8.9 | all-reduce | flops 2 | bytes 16 | tf_op jit(solution)/shard_map/psum | solution.py:39
  100.9 17.5 %all-reduce.16 = (f32[]{:T(128)}, f32[]{:T(128)}) all-reduce(f32[]{:T(128)} %get-tuple-element.5, f32[]{:T(128)} %get-tuple-element.6), channel_id=1, replica_groups=mesh['mem_0'=2,'mem_1'=4,'tile_0'=8,'tile_1'=2,'tile_2'=2] {'tile_0'}, use_global_device_ids=true, to_apply=%region_9.10 | all-reduce | flops 2 | bytes 16 | tf_op jit(solution)/shard_map/psum | solution.py:39
  118.3 7.1 %all-reduce.19 = (f32[]{:T(128)}, f32[]{:T(128)}) all-reduce(f32[]{:T(128)} %get-tuple-element.3, f32[]{:T(128)} %get-tuple-element.4), channel_id=1, replica_groups=mesh['mem_0'=2,'mem_1'=4,'tile_0'=8,'tile_1'=2,'tile_2'=2] {'tile_1'}, use_global_device_ids=true, to_apply=%region_10.11 | all-reduce | flops 2 | bytes 16 | tf_op jit(solution)/shard_map/psum | solution.py:39
  125.4 13.6 %all-reduce.18 = (f32[]{:T(128)}, f32[]{:T(128)}) all-reduce(f32[]{:T(128)} %get-tuple-element.9, f32[]{:T(128)} %get-tuple-element.10), channel_id=1, replica_groups=mesh['mem_0'=2,'mem_1'=4,'tile_0'=8,'tile_1'=2,'tile_2'=2] {'tile_2'}, use_global_device_ids=true, to_apply=%region_11.12 | all-reduce | flops 2 | bytes 16 | tf_op jit(solution)/shard_map/psum | solution.py:39
  141.0 0.2 pad_maximum_fusion.3
  141.3 0.7 broadcast_multiply_fusion.12
  142.1 0.7 broadcast_multiply_fusion.8
  143.0 0.7 broadcast_multiply_fusion.4
  143.8 1.3 fusion.123
  (72 shorter events, 2.9 us)
Async XLA Ops:
  0.6 23.5 %copy-start.2 = (f32[32,16,256]{2,1,0:T(8,128)S(1)}, f32[32,16,256]{2,1,0:T(8,128)}, u32[]{:S(2)}) copy-start(f32[32,16,256]{2,1,0:T(8,128)} %param.8) | copy-start | bytes 1572868
  2.2 16.4 %collective-permute-start.2 = (f32[3,4,256]{2,1,0:T(4,128)S(1)}, f32[3,4,256]{2,1,0:T(4,128)S(1)}, u32[]{:S(2)}, u32[]{:S(2)}) collective-permute-start(f32[3,4,256]{2,1,0:T(4,128)S(1)} %get-tuple-element.51), channel_id=1, source_target_pairs={{0,1},{1,2},{2,3},{3,4},{4,5},{5,6},{6,7},{7,8},{8,9},{9,10},{10,1... | collective-permute-start | bytes 36872 | tf_op jit(solution)/shard_map/ppermute | solution.py:20
  8.2 10.4 %collective-permute-start.3 = (f32[3,4,256]{2,1,0:T(4,128)S(1)}, f32[3,4,256]{2,1,0:T(4,128)S(1)}, u32[]{:S(2)}, u32[]{:S(2)}) collective-permute-start(f32[3,4,256]{2,1,0:T(4,128)S(1)} %get-tuple-element.52), channel_id=1, source_target_pairs={{1,0},{2,1},{3,2},{4,3},{5,4},{6,5},{7,6},{8,7},{9,8},{10,9},{11,1... | collective-permute-start | bytes 36872 | tf_op jit(solution)/shard_map/ppermute | solution.py:23
  11.2 8.3 %collective-permute-start = (f32[32,4,256]{2,1,0:T(4,128)S(1)}, f32[32,4,256]{2,1,0:T(4,128)S(1)}, u32[]{:S(2)}, u32[]{:S(2)}) collective-permute-start(f32[32,4,256]{2,1,0:T(4,128)S(1)} %get-tuple-element.41), channel_id=1, source_target_pairs={{0,1},{1,2},{2,3},{3,4},{4,5},{5,6},{6,7},{7,8},{8,9},{9,10},{10,1... | collective-permute-start | bytes 393224 | tf_op jit(solution)/shard_map/ppermute | solution.py:20
  16.4 7.8 %collective-permute-start.1 = (f32[32,4,256]{2,1,0:T(4,128)S(1)}, f32[32,4,256]{2,1,0:T(4,128)S(1)}, u32[]{:S(2)}, u32[]{:S(2)}) collective-permute-start(f32[32,4,256]{2,1,0:T(4,128)S(1)} %get-tuple-element.42), channel_id=1, source_target_pairs={{1,0},{2,1},{3,2},{4,3},{5,4},{6,5},{7,6},{8,7},{9,8},{10,9},{11,1... | collective-permute-start | bytes 393224 | tf_op jit(solution)/shard_map/ppermute | solution.py:23
  26.6 0.7 copy-start.3
  26.6 0.7 copy-start.4
  27.4 1.1 copy-start
  29.5 11.0 %copy-start.5 = (f32[3,16,256]{2,1,0:T(8,128)S(1)}, f32[3,16,256]{2,1,0:T(8,128)}, u32[]{:S(2)}) copy-start(f32[3,16,256]{2,1,0:T(8,128)} %param.10) | copy-start | bytes 147460
  29.5 11.0 %copy-start.6 = (f32[3,16,256]{2,1,0:T(8,128)S(1)}, f32[3,16,256]{2,1,0:T(8,128)}, u32[]{:S(2)}) copy-start(f32[3,16,256]{2,1,0:T(8,128)} %param.9) | copy-start | bytes 147460
  29.5 11.0 %all-to-all-start = ((f32[8,3,16,256]{3,2,1,0:T(8,128)}), f32[8,3,16,256]{3,2,1,0:T(8,128)S(1)}, u32[]{:S(2)}, u32[]{:S(2)}) async-start(f32[8,3,16,256]{3,2,1,0:T(8,128)} %broadcast_in_dim.86), calls=%async_computation | async-start | bytes 786432 | tf_op jit(solution)/shard_map/all_to_all | solution.py:30
  40.7 5.8 %collective-permute-start.4 = (f32[32,4,256]{2,1,0:T(4,128)S(1)}, f32[32,4,256]{2,1,0:T(4,128)S(1)}, u32[]{:S(2)}, u32[]{:S(2)}) collective-permute-start(f32[32,4,256]{2,1,0:T(4,128)S(1)} %get-tuple-element.39), channel_id=1, source_target_pairs={{0,1},{1,2},{2,3},{3,4},{4,5},{5,6},{6,7},{7,8},{8,9},{9,10},{10,1... | collective-permute-start | bytes 393224 | tf_op jit(solution)/shard_map/ppermute | solution.py:20
  44.5 7.9 %collective-permute-start.5 = (f32[32,4,256]{2,1,0:T(4,128)S(1)}, f32[32,4,256]{2,1,0:T(4,128)S(1)}, u32[]{:S(2)}, u32[]{:S(2)}) collective-permute-start(f32[32,4,256]{2,1,0:T(4,128)S(1)} %get-tuple-element.40), channel_id=1, source_target_pairs={{1,0},{2,1},{3,2},{4,3},{5,4},{6,5},{7,6},{8,7},{9,8},{10,9},{11,1... | collective-permute-start | bytes 393224 | tf_op jit(solution)/shard_map/ppermute | solution.py:23
  56.4 87.4 %copy-start.1 = (f32[32,16,256]{2,1,0:T(8,128)}, f32[32,16,256]{2,1,0:T(8,128)S(1)}, u32[]{:S(2)}) copy-start(f32[32,16,256]{2,1,0:T(8,128)S(1)} %get-tuple-element.16) | copy-start | bytes 1572868
  56.5 4.3 %collective-permute-start.6 = (f32[32,4,256]{2,1,0:T(4,128)S(1)}, f32[32,4,256]{2,1,0:T(4,128)S(1)}, u32[]{:S(2)}, u32[]{:S(2)}) collective-permute-start(f32[32,4,256]{2,1,0:T(4,128)S(1)} %get-tuple-element.37), channel_id=1, source_target_pairs={{0,1},{1,2},{2,3},{3,4},{4,5},{5,6},{6,7},{7,8},{8,9},{9,10},{10,1... | collective-permute-start | bytes 393224 | tf_op jit(solution)/shard_map/ppermute | solution.py:20
  58.5 10.5 %collective-permute-start.7 = (f32[32,4,256]{2,1,0:T(4,128)S(1)}, f32[32,4,256]{2,1,0:T(4,128)S(1)}, u32[]{:S(2)}, u32[]{:S(2)}) collective-permute-start(f32[32,4,256]{2,1,0:T(4,128)S(1)} %get-tuple-element.38), channel_id=1, source_target_pairs={{1,0},{2,1},{3,2},{4,3},{5,4},{6,5},{7,6},{8,7},{9,8},{10,9},{11,1... | collective-permute-start | bytes 393224 | tf_op jit(solution)/shard_map/ppermute | solution.py:23
  82.6 58.4 %collective-permute-start.8 = (f32[32,4,256]{2,1,0:T(4,128)S(1)}, f32[32,4,256]{2,1,0:T(4,128)S(1)}, u32[]{:S(2)}, u32[]{:S(2)}) collective-permute-start(f32[32,4,256]{2,1,0:T(4,128)S(1)} %get-tuple-element.35), channel_id=1, source_target_pairs={{0,1},{1,2},{2,3},{3,4},{4,5},{5,6},{6,7},{7,8},{8,9},{9,10},{10,1... | collective-permute-start | bytes 393224 | tf_op jit(solution)/shard_map/ppermute | solution.py:20
  86.4 54.6 %collective-permute-start.9 = (f32[32,4,256]{2,1,0:T(4,128)S(1)}, f32[32,4,256]{2,1,0:T(4,128)S(1)}, u32[]{:S(2)}, u32[]{:S(2)}) collective-permute-start(f32[32,4,256]{2,1,0:T(4,128)S(1)} %get-tuple-element.36), channel_id=1, source_target_pairs={{1,0},{2,1},{3,2},{4,3},{5,4},{6,5},{7,6},{8,7},{9,8},{10,9},{11,1... | collective-permute-start | bytes 393224 | tf_op jit(solution)/shard_map/ppermute | solution.py:23
where the time goes:
time: 147 us; the launch traced here: 146 us
  blocking collectives  59.6 us (41%)
  starting transfers between devices  35.2 us (24%)
  waiting for transfers between devices  25.3 us (17%)
  other arithmetic  16.5 us (11%)
  between operations  4.98 us (3%)
  local copies, waits for them, and re-layouts  4.84 us (3%)
    psum x5, blocking collectives, over_axes(): return functools.reduce(lax.psum, axes, x)  50 us
    ppermute x5, starting transfers between devices, extended_2(): lax.ppermute(lax.slice_in_dim(block, block.shape[dim] - width, None, axis...  20.8 us
    ppermute x5, waiting for transfers between devices, extended_2(): lax.ppermute(lax.slice_in_dim(block, 0, width, axis=dim), axis, backward)  18.7 us
    ppermute x5, starting transfers between devices, extended_2(): lax.ppermute(lax.slice_in_dim(block, 0, width, axis=dim), axis, backward)  10 us
    all_to_all x1, blocking collectives, sent_to_all(): lax.all_to_all(jnp.broadcast_to(x[None], (devices, *x.shape)), axis, 0, 0...  9.57 us
    all_to_all x1, waiting for transfers between devices, sent_to_all(): lax.all_to_all(jnp.broadcast_to(x[None], (devices, *x.shape)), axis, 0, 0...  6.58 us
    mul x8, other arithmetic, localise(): forward_core(extended, kappa_wide[first_row:last_row], advect_wide[first_...  5.07 us
    all_to_all x1, starting transfers between devices, sent_to_all(): lax.all_to_all(jnp.broadcast_to(x[None], (devices, *x.shape)), axis, 0, 0...  4.35 us
  transfers between devices with their start and end apart: 11, of which 4 were waited for; matrix products, arithmetic and copies ran while one was open for 2% of the time, Pallas kernels for 0%

commit v1 on v0

v1 whole, which is shorter than its diff:
```python
import functools

import jax
import jax.numpy as jnp
from jax import lax
from jax.experimental import pallas as pl
from jax.experimental.pallas import tpu as pltpu
from jax.sharding import PartitionSpec as P

MESH = pl.DeviceIdType.MESH
SUB = 8
LANES = 128
HALVES = 2
NT = 3
ROWS = 16
MEMBERS = 32
GROUPS = MEMBERS // SUB
MEM_COUNT = 8
TILE_COUNT = 32
WIDE = 8
EXT = ROWS + 2 * WIDE
NEAR = 4
FORWARD = 0
ADJOINT = 5


def kernel(
    ctrl,
    pert,
    innov,
    weight,
    diff,
    adv,
    upw,
    grad_out,
    hess_out,
    step_out,
    ctrl_nat,
    pert_half,
    pert_nat,
    pert_t,
    small_in,
    upw_in,
    obs_in,
    raw,
    coef,
    field,
    ping,
    pong,
    pulled,
    grad,
    pulled_2,
    edge_1,
    mid_1,
    edge_2,
    mid_2,
    mis,
    scal,
    grad_nat,
    hess_nat,
    in_sem,
    out_sem,
    halo_send,
    halo_recv,
    red_send,
    red_recv,
    scal_send,
    scal_recv,
):
    t = lax.axis_index("tile")
    m = lax.axis_index("mem")
    nxt = lax.rem(t + 1, TILE_COUNT)
    prv = lax.rem(t + TILE_COUNT - 1, TILE_COUNT)

    barrier = pltpu.get_barrier_semaphore()

    def greet_tile(k, c):
        pl.semaphore_signal(
            barrier, inc=1, device_id=(m, lax.rem(t + k, TILE_COUNT)), device_id_type=MESH
        )
        return c

    lax.fori_loop(1, TILE_COUNT, greet_tile, 0)
    for k in range(1, MEM_COUNT):
        pl.semaphore_signal(
            barrier, inc=1, device_id=(lax.rem(m + k, MEM_COUNT), t), device_id_type=MESH
        )

    loads = []
    for h in range(HALVES):
        cols = pl.ds(h * LANES, LANES)
        loads.append((ctrl.at[:, cols], ctrl_nat.at[h]))
        loads.append((diff.at[:, cols], small_in.at[0, h]))
        loads.append((adv.at[:, cols], small_in.at[1, h]))
        loads.append((upw.at[:, cols], upw_in.at[h]))
        loads.append((innov.at[:, cols], obs_in.at[0, h]))
        loads.append((weight.at[:, cols], obs_in.at[1, h]))
    loads.append((pert, pert_half))
    loads = [
        pltpu.make_async_copy(src, dst, in_sem.at[n]) for n, (src, dst) in enumerate(loads)
    ]
    for copy in loads:
        copy.start()

    lane = lax.broadcasted_iota(jnp.int32, (SUB, LANES), 1)
    low_sub = lax.broadcasted_iota(jnp.int32, (SUB, LANES), 0) < SUB // 2
    at_last = lane == LANES - 1
    at_first = lane == 0

    for copy in loads[:-1]:
        copy.wait()

    def place_control(r, c):
        for h in range(HALVES):
            for g in range(GROUPS):
                field[r + NEAR, h, pl.ds(SUB * g, SUB), :] = ctrl_nat[
                    h, pl.ds(SUB * g * ROWS + r, SUB, stride=ROWS), :
                ]
        return c

    lax.fori_loop(0, ROWS, place_control, 0, unroll=2)
    for h in range(HALVES):
        raw[0, h, pl.ds(WIDE, ROWS), :] = small_in[0, h]
        raw[1, h, pl.ds(WIDE, ROWS), :] = small_in[1, h]
        raw[2, h, pl.ds(WIDE, ROWS), :] = jnp.where(upw_in[h] == 1, 1.0, 0.0)

    def to_neighbours(buffer, own, depth, first):
        copies = []
        for n, (src_row, dst_row, dest) in enumerate(
            ((own, own + ROWS, prv), (own + ROWS - depth, own - depth, nxt))
        ):
            copies.append(
                pltpu.make_async_remote_copy(
                    src_ref=buffer(src_row, depth),
                    dst_ref=buffer(dst_row, depth),
                    send_sem=halo_send.at[first + n],
                    recv_sem=halo_recv.at[first + n],
                    device_id=(m, dest),
                    device_id_type=MESH,
                )
            )
        for copy in copies:
            copy.start()
        return copies

    def rows_of(ref):
        return lambda start, count: ref.at[pl.ds(start, count)]

    pl.semaphore_wait(barrier, TILE_COUNT - 1 + MEM_COUNT - 1)

    coef_copies = to_neighbours(
        lambda start, count: raw.at[:, :, pl.ds(start, count), :], WIDE, WIDE, 0
    )
    ctrl_copies = to_neighbours(rows_of(field), NEAR, NEAR, 2)

    loads[-1].wait()

    def widen(q, c):
        rows = pl.ds(pl.multiple_of(q * ROWS, ROWS), ROWS)
        for h in range(HALVES):
            pert_nat[h, rows, :] = pert_half[rows, pl.ds(h * LANES, LANES)].astype(jnp.float32)
        return c

    lax.fori_loop(0, NT * MEMBERS, widen, 0, unroll=4)

    def place_pert(r, c):
        for n in range(NT):
            for h in range(HALVES):
                for g in range(GROUPS):
                    pert_t[n, r, h, pl.ds(SUB * g, SUB), :] = pert_nat[
                        h, pl.ds((n * MEMBERS + SUB * g) * ROWS + r, SUB, stride=ROWS), :
                    ]
        return c

    lax.fori_loop(0, ROWS, place_pert, 0)

    for copy in coef_copies:
        copy.wait()

    row = lax.broadcasted_iota(jnp.int32, (EXT, LANES), 0)
    col = lax.broadcasted_iota(jnp.int32, (EXT, LANES), 1)
    top = jnp.logical_and(row == WIDE, t == 0)
    bottom = jnp.logical_and(row == WIDE + ROWS - 1, t == TILE_COUNT - 1)
    kappa = [raw[0, h] for h in range(HALVES)]
    right = [pltpu.roll(k, LANES - 1, 1) for k in kappa]
    left = [pltpu.roll(k, 1, 1) for k in kappa]
    right = [jnp.where(col == LANES - 1, right[1], right[0]), jnp.where(col == LANES - 1, 0.0, right[1])]
    left = [jnp.where(col == 0, 0.0, left[0]), jnp.where(col == 0, left[0], left[1])]
    for h in range(HALVES):
        k = kappa[h]
        a = raw[1, h]
        u = raw[2, h]
        centre = 1.0 - 4.0 * k - a
        below = k + a * u
        above = k + a * (1.0 - u)
        edge_right = jnp.logical_and(col == LANES - 1, h == HALVES - 1)
        edge_left = jnp.logical_and(col == 0, h == 0)
        coef[FORWARD + 0, h] = centre
        coef[FORWARD + 1, h] = jnp.where(bottom, 0.0, below)
        coef[FORWARD + 2, h] = jnp.where(top, 0.0, above)
        coef[FORWARD + 3, h] = jnp.where(edge_right, 0.0, k)
        coef[FORWARD + 4, h] = jnp.where(edge_left, 0.0, k)
        coef[ADJOINT + 0, h] = centre
        coef[ADJOINT + 1, h] = jnp.where(bottom, 0.0, pltpu.roll(above, EXT - 1, 0))
        coef[ADJOINT + 2, h] = jnp.where(top, 0.0, pltpu.roll(below, 1, 0))
        coef[ADJOINT + 3, h] = right[h]
        coef[ADJOINT + 4, h] = left[h]

    def sweep(src, src_own, dst, dst_own, kind, first, last, add=None, add_own=0):
        def two_rows(i, c):
            r = first + 2 * i
            factor = [
                [
                    [
                        coef[kind + n, h, pl.ds(r + d + WIDE, SUB, stride=0), :]
                        for h in range(HALVES)
                    ]
                    for n in range(5)
                ]
                for d in range(2)
            ]
            for g in range(GROUPS):
                part = pl.ds(SUB * g, SUB)
                lines = [
                    [src[r + src_own + d, h, part, :] for h in range(HALVES)]
                    for d in range(-1, 3)
                ]
                for d in range(2):
                    above, centre, below = lines[d], lines[d + 1], lines[d + 2]
                    right = [pltpu.roll(x, LANES - 1, 1) for x in centre]
                    left = [pltpu.roll(x, 1, 1) for x in centre]
                    right = [jnp.where(at_last, right[1], right[0]), right[1]]
                    left = [left[0], jnp.where(at_first, left[0], left[1])]
                    for h in range(HALVES):
                        f = [factor[d][n][h] for n in range(5)]
                        value = (f[0] * centre[h] + f[1] * below[h]) + (
                            f[2] * above[h] + (f[3] * right[h] + f[4] * left[h])
                        )
                        if add is not None:
                            value = value + add[r + d + add_own, h, part, :]
                        dst[r + d + dst_own, h, part, :] = value
            return c

        lax.fori_loop(0, (last - first) // 2, two_rows, 0)

    def four_sweeps(src, src_own, dst, dst_own, kind, margin, add=None, add_own=0):
        steps = ((src, src_own), (ping, WIDE), (pong, WIDE), (ping, WIDE), (dst, dst_own))
        for n in range(4):
            reach = margin - 1 - n
            source, source_own = steps[n]
            target, target_own = steps[n + 1]
            sweep(
                source,
                source_own,
                target,
                target_own,
                kind,
                -reach,
                ROWS + reach,
                add if n == 3 else None,
                add_own,
            )

    def project(src, src_own, out, upper, lower):
        def body(s, c):
            for base, sub in ((upper, 0), (lower, SUB // 2)):
                for h in range(HALVES):
                    value = [
                        src[base + s + src_own, h, pl.ds(SUB * g, SUB), :] for g in range(GROUPS)
                    ]
                    for n in range(NT):
                        total = value[0] * pert_t[n, base + s, h, pl.ds(0, SUB), :]
                        for g in range(1, GROUPS):
                            total = (
                                total + value[g] * pert_t[n, base + s, h, pl.ds(SUB * g, SUB), :]
                            )
                        out[m, HALVES * n + h, pl.ds(s + sub, 1), :] = jnp.sum(
                            total, axis=0, keepdims=True
                        )
            return c

        lax.fori_loop(0, SUB // 2, body, 0)

    def to_members(out, first):
        copies = []
        for k in range(1, MEM_COUNT):
            copies.append(
                pltpu.make_async_remote_copy(
                    src_ref=out.at[m],
                    dst_ref=out.at[m],
                    send_sem=red_send.at[first, k],
                    recv_sem=red_recv.at[first, k],
                    device_id=(lax.rem(m + k, MEM_COUNT), t),
                    device_id_type=MESH,
                )
            )
        for copy in copies:
            copy.start()
        return copies

    def wait_members(out, first):
        for k in range(1, MEM_COUNT):
            pltpu.make_async_remote_copy(
                src_ref=out.at[m],
                dst_ref=out.at[lax.rem(m + MEM_COUNT - k, MEM_COUNT)],
                send_sem=red_send.at[first, k],
                recv_sem=red_recv.at[first, k],
                device_id=(lax.rem(m + k, MEM_COUNT), t),
                device_id_type=MESH,
            ).wait_recv()

    def total_of(out, index):
        total = out[0, index]
        for k in range(1, MEM_COUNT):
            total = total + out[k, index]
        return total

    def observed(which, h, n, edge):
        upper = obs_in[which, h, pl.ds(ROWS * n, SUB), :]
        lower = obs_in[which, h, pl.ds(ROWS * n + SUB, SUB), :]
        return jnp.where(low_sub, upper, lower) if edge else jnp.where(low_sub, lower, upper)

    def pull_back(dst, dst_own, block, upper, lower):
        def body(s, c):
            for base, sub in ((upper, 0), (lower, SUB // 2)):
                for h in range(HALVES):
                    w = [
                        mis[block, HALVES * n + h, pl.ds(s + sub, SUB, stride=0), :]
                        for n in range(NT)
                    ]
                    for g in range(GROUPS):
                        part = pl.ds(SUB * g, SUB)
                        value = w[0] * pert_t[0, base + s, h, part, :]
                        for n in range(1, NT):
                            value = value + w[n] * pert_t[n, base + s, h, part, :]
                        dst[base + s + dst_own, h, part, :] = value
            return c

        lax.fori_loop(0, SUB // 2, body, 0)

    for copy in ctrl_copies:
        copy.wait()

    four_sweeps(field, NEAR, pong, WIDE, FORWARD, NEAR)
    project(pong, WIDE, edge_1, 0, 12)
    sent_e1 = to_members(edge_1, 0)
    project(pong, WIDE, mid_1, 8, 4)
    sent_m1 = to_members(mid_1, 1)
    for block, out, upper, lower in ((0, edge_1, 0, 12), (1, mid_1, 8, 4)):
        wait_members(out, block)
        for n in range(NT):
            for h in range(HALVES):
                mis[block, HALVES * n + h] = observed(1, h, n, block == 0) * (
                    total_of(out, HALVES * n + h) - observed(0, h, n, block == 0)
                )
        pull_back(pulled, WIDE, block, upper, lower)

    pull_copies = to_neighbours(rows_of(pulled), WIDE, WIDE, 4)
    for copy in pull_copies:
        copy.wait()
    four_sweeps(pulled, WIDE, grad, NEAR, ADJOINT, WIDE, add=field, add_own=NEAR)

    def square(r, total):
        for h in range(HALVES):
            for g in range(GROUPS):
                x = grad[r + NEAR, h, pl.ds(SUB * g, SUB), :]
                grad_nat[h, pl.ds(SUB * g * ROWS + r, SUB, stride=ROWS), :] = x
                total = total + x * x
        return total

    edge_2[m, NT * HALVES] = lax.fori_loop(
        0, ROWS, square, jnp.zeros((SUB, LANES), jnp.float32)
    )
    stores = [
        pltpu.make_async_copy(
            grad_nat.at[h], grad_out.at[:, pl.ds(h * LANES, LANES)], out_sem.at[h]
        )
        for h in range(HALVES)
    ]
    for copy in stores:
        copy.start()

    four_sweeps(grad, NEAR, pong, WIDE, FORWARD, NEAR)
    project(pong, WIDE, edge_2, 0, 12)
    sent_e2 = to_members(edge_2, 2)
    project(pong, WIDE, mid_2, 8, 4)
    sent_m2 = to_members(mid_2, 3)
    observed_sum = jnp.zeros((SUB, LANES), jnp.float32)
    last_copies = []
    for block, out, upper, lower in ((0, edge_2, 0, 12), (1, mid_2, 8, 4)):
        wait_members(out, 2 + block)
        for n in range(NT):
            for h in range(HALVES):
                image = total_of(out, HALVES * n + h)
                weighted = observed(1, h, n, block == 0) * image
                mis[2 + block, HALVES * n + h] = weighted
                observed_sum = observed_sum + image * weighted
        pull_back(pulled_2, NEAR, 2 + block, upper, lower)
        if block == 0:
            last_copies = to_neighbours(rows_of(pulled_2), NEAR, NEAR, 6)
    squares = total_of(edge_2, NT * HALVES)

    scal[t] = jnp.where(
        low_sub,
        jnp.broadcast_to(jnp.sum(squares, axis=0, keepdims=True), (SUB, LANES)),
        jnp.broadcast_to(jnp.sum(observed_sum, axis=0, keepdims=True), (SUB, LANES)),
    )

    def scalar_copy(k, slot):
        return pltpu.make_async_remote_copy(
            src_ref=scal.at[t],
            dst_ref=scal.at[slot],
            send_sem=scal_send.at[k],
            recv_sem=scal_recv.at[k],
            device_id=(m, lax.rem(t + k, TILE_COUNT)),
            device_id_type=MESH,
        )

    def send_scalar(k, c):
        scalar_copy(k, t).start()
        return c

    lax.fori_loop(1, TILE_COUNT, send_scalar, 0)

    for copy in last_copies:
        copy.wait()
    four_sweeps(pulled_2, NEAR, pong, WIDE, ADJOINT, NEAR, add=grad, add_own=NEAR)

    def place_hess(r, c):
        for h in range(HALVES):
            for g in range(GROUPS):
                hess_nat[h, pl.ds(SUB * g * ROWS + r, SUB, stride=ROWS), :] = pong[
                    r + WIDE, h, pl.ds(SUB * g, SUB), :
                ]
        return c

    lax.fori_loop(0, ROWS, place_hess, 0, unroll=2)
    for h in range(HALVES):
        copy = pltpu.make_async_copy(
            hess_nat.at[h], hess_out.at[:, pl.ds(h * LANES, LANES)], out_sem.at[HALVES + h]
        )
        copy.start()
        stores.append(copy)

    def wait_scalar(k, c):
        copy = scalar_copy(k, lax.rem(t + TILE_COUNT - k, TILE_COUNT))
        copy.wait_recv()
        copy.wait_send()
        return c

    lax.fori_loop(1, TILE_COUNT, wait_scalar, 0)
    sums = lax.fori_loop(
        0, TILE_COUNT, lambda k, s: s + scal[k], jnp.zeros((SUB, LANES), jnp.float32)
    )
    both = jnp.sum(sums, axis=1, keepdims=True)
    all_squares = both[0:1]
    step_out[...] = all_squares / (all_squares + both[SUB // 2 : SUB // 2 + 1])

    for copies in (sent_e1, sent_m1, sent_e2, sent_m2):
        for copy in copies:
            copy.wait_send()
    for copy in stores:
        copy.wait()


def shards(perturbations, control, innovation, obs_weight, diffusion, advection, upwind):
    f32 = jnp.float32
    cells = MEMBERS * ROWS
    width = HALVES * LANES
    any_space = pl.BlockSpec(memory_space=pl.ANY)

    def lines(count):
        return pltpu.VMEM((count, HALVES, MEMBERS, LANES), f32)

    def sums(count):
        return pltpu.VMEM((MEM_COUNT, count, SUB, LANES), f32)

    gradient, hessian, step = pl.pallas_call(
        kernel,
        out_shape=(
            jax.ShapeDtypeStruct((cells, width), f32),
            jax.ShapeDtypeStruct((cells, width), f32),
            jax.ShapeDtypeStruct((1, 1), f32),
        ),
        in_specs=[any_space] * 7,
        out_specs=(any_space, any_space, pl.BlockSpec(memory_space=pltpu.VMEM)),
        scratch_shapes=[
            pltpu.VMEM((HALVES, cells, LANES), f32),
            pltpu.VMEM((NT * cells, width), jnp.bfloat16),
            pltpu.VMEM((HALVES, NT * cells, LANES), f32),
            pltpu.VMEM((NT, ROWS, HALVES, MEMBERS, LANES), f32),
            pltpu.VMEM((2, HALVES, ROWS, LANES), f32),
            pltpu.VMEM((HALVES, ROWS, LANES), jnp.int32),
            pltpu.VMEM((2, HALVES, NT * ROWS, LANES), f32),
            pltpu.VMEM((3, HALVES, EXT, LANES), f32),
            pltpu.VMEM((10, HALVES, EXT, LANES), f32),
            lines(ROWS + 2 * NEAR),
            lines(EXT),
            lines(EXT),
            lines(EXT),
            lines(ROWS + 2 * NEAR),
            lines(ROWS + 2 * NEAR),
            sums(NT * HALVES),
            sums(NT * HALVES),
            sums(NT * HALVES + 1),
            sums(NT * HALVES),
            pltpu.VMEM((4, NT * HALVES, SUB, LANES), f32),
            pltpu.VMEM((TILE_COUNT, SUB, LANES), f32),
            pltpu.VMEM((HALVES, cells, LANES), f32),
            pltpu.VMEM((HALVES, cells, LANES), f32),
            pltpu.SemaphoreType.DMA((13,)),
            pltpu.SemaphoreType.DMA((4,)),
            pltpu.SemaphoreType.DMA((8,)),
            pltpu.SemaphoreType.DMA((8,)),
            pltpu.SemaphoreType.DMA((4, MEM_COUNT)),
            pltpu.SemaphoreType.DMA((4, MEM_COUNT)),
            pltpu.SemaphoreType.DMA((TILE_COUNT,)),
            pltpu.SemaphoreType.DMA((TILE_COUNT,)),
        ],
        compiler_params=pltpu.CompilerParams(
            collective_id=0, has_side_effects=True, vmem_limit_bytes=63 << 20
        ),
    )(
        control.reshape(cells, width),
        perturbations.reshape(NT * cells, width),
        innovation.reshape(NT * ROWS, width),
        obs_weight.reshape(NT * ROWS, width),
        diffusion,
        advection,
        upwind,
    )
    return (
        gradient.reshape(control.shape),
        hessian.reshape(control.shape),
        step.reshape(()),
    )


def solution(mesh):
    return jax.shard_map(
        shards,
        mesh=mesh,
        in_specs=(
            P(None, "mem", "tile", None),
            P("mem", "tile", None),
            P(None, "tile", None),
            P(None, "tile", None),
            P("tile", None),
            P("tile", None),
            P("tile", None),
        ),
        out_specs=(P("mem", "tile", None), P("mem", "tile", None), P()),
        check_vma=False,
    )
```

time: 147 us -> 68.8 us (0.47)
  Pallas kernels: 0 us -> 63.6 us
  blocking collectives: 59.6 us -> 0 us
  starting transfers between devices: 35.2 us -> 0 us
  waiting for transfers between devices: 25.3 us -> 0 us
  other arithmetic: 16.5 us -> 0 us
  between operations: 4.98 us -> 2.41 us
  local copies, waits for them, and re-layouts: 4.84 us -> 2.72 us
    pallas_call x0 -> x1, Pallas kernels: none -> 63.6 us  [shards(): pl.pallas_call(kernel, out_shape=(jax.ShapeDtypeStruct((cells, width), f3...]
    psum x5 -> x0, blocking collectives: 50 us -> none  [over_axes(): return functools.reduce(lax.psum, axes, x)]
    ppermute x10 -> x0, starting transfers between devices: 30.8 us -> none  [the longest x5 20.8 us: extended_2(): lax.ppermute(lax.slice_in_dim(block, block.shape[dim] - width, None, axis...]
    ppermute x10 -> x0, waiting for transfers between devices: 18.7 us -> none  [the longest x5 18.7 us: extended_2(): lax.ppermute(lax.slice_in_dim(block, 0, width, axis=dim), axis, backward)]
    mul x21 -> x0, other arithmetic: 9.7 us -> none  [the longest x8 5.07 us: localise(): forward_core(extended, kappa_wide[first_row:last_row], advect_wide[first_...]
    all_to_all x1 -> x0, blocking collectives: 9.57 us -> none  [sent_to_all(): lax.all_to_all(jnp.broadcast_to(x[None], (devices, *x.shape)), axis, 0, 0...]
    all_to_all x1 -> x0, waiting for transfers between devices: 6.58 us -> none  [sent_to_all(): lax.all_to_all(jnp.broadcast_to(x[None], (devices, *x.shape)), axis, 0, 0...]
    all_to_all x1 -> x0, starting transfers between devices: 4.35 us -> none  [sent_to_all(): lax.all_to_all(jnp.broadcast_to(x[None], (devices, *x.shape)), axis, 0, 0...]
  transfers between devices with their start and end apart: 11 -> 0, of which waited for: 4 -> 0; matrix products, arithmetic and copies ran while one was open for 2% -> 0% of each run, Pallas kernels for 0% -> 0%
where the time goes in v1:
time: 68.8 us; the launch traced here: 68.7 us
  Pallas kernels  63.6 us (92%)
  local copies, waits for them, and re-layouts  2.72 us (4%)
  between operations  2.41 us (4%)
    pallas_call x1, Pallas kernels, shards(): pl.pallas_call(kernel, out_shape=(jax.ShapeDtypeStruct((cells, width), f3...  63.6 us
    unnamed x4, local copies, waits for them, and re-layouts  2.72 us

profile of v1, /device:TPU:1, one launch (start us, length us, event | category | flops | bytes accessed | tf_op | source)
XLA Modules:
  0.0 68.7 jit_solution(13804844489924650237)
XLA Ops:
  0.6 63.6 %shard_map.94 = (f32[512,256]{1,0:T(8,128)}, f32[512,256]{1,0:T(8,128)}, f32[1,1]{1,0:T(1,128)}) custom-call(f32[512,256]{1,0:T(8,128)} %bitcast.10, bf16[1536,256]{1,0:T(8,128)(2,1)} %bitcast.7, f32[48,256]{1,0:T(8,128)} %bitcast.11, f32[48,256]{1,0:T(8,128)} %bitcast.12, f32[16,256]{1,0:T(8,128)} %diff.1, f32[16,256]{1,0:T(8,128)} %adv.1, s32[16,256]{1,0:T(8,128)} %upw.1), custom_call_target="tpu_custom_call" | custom-call | tf_op jit(solution)/shard_map/pallas_call | solution.py:478
  64.2 0.0 copy-start
  64.2 1.9 %copy.13 = f32[32,16,256]{2,1,0:T(8,128)} copy(f32[32,16,256]{2,1,0:T(8,128)} %bitcast.9) | data formatting | bytes 1048576
  66.1 0.0 copy-done
  66.1 0.8 %copy.14 = f32[32,16,256]{2,1,0:T(8,128)} copy(f32[32,16,256]{2,1,0:T(8,128)S(1)} %bitcast.8) | data formatting | bytes 1048576
Async XLA Ops:
  64.2 1.9 %copy-start = (f32[512,256]{1,0:T(8,128)S(1)}, f32[512,256]{1,0:T(8,128)}, u32[]{:S(2)}) copy-start(f32[512,256]{1,0:T(8,128)} %get-tuple-element.7) | copy-start | bytes 1572868

commit v2 on v1

v2 whole, which is shorter than its diff:
```python
import functools

import jax
import jax.numpy as jnp
from jax import lax
from jax.experimental import pallas as pl
from jax.experimental.pallas import tpu as pltpu
from jax.sharding import PartitionSpec as P

MESH = pl.DeviceIdType.MESH
SUB = 8
LANES = 128
HALVES = 2
NT = 3
ROWS = 16
MEMBERS = 32
GROUPS = MEMBERS // SUB
MEM_COUNT = 8
TILE_COUNT = 32
WIDE = 8
EXT = ROWS + 2 * WIDE
NEAR = 4
PLANE = 4
FORWARD = 0
ADJOINT = 5


def kernel(
    ctrl,
    pert,
    innov,
    weight,
    diff,
    adv,
    upw,
    grad_out,
    hess_out,
    step_out,
    ctrl_nat,
    pert_half,
    pert_nat,
    pert_t,
    small_in,
    upw_in,
    obs_in,
    raw,
    coef,
    field,
    level_1,
    level_2,
    level_3,
    pulled,
    grad,
    pulled_2,
    result,
    edge_1,
    mid_1,
    edge_2,
    mid_2,
    mis,
    scal,
    grad_nat,
    hess_nat,
    in_sem,
    out_sem,
    halo_send,
    halo_recv,
    red_send,
    red_recv,
    scal_send,
    scal_recv,
    known_sem,
):
    t = lax.axis_index("tile")
    m = lax.axis_index("mem")

    def tile_at(k):
        return lax.rem(t + k + TILE_COUNT, TILE_COUNT)

    barrier = pltpu.get_barrier_semaphore()
    near = [tile_at(1), tile_at(-1), tile_at(PLANE), tile_at(-PLANE)]
    near += [(t // PLANE) * PLANE + lax.rem(t + k, PLANE) for k in range(1, PLANE)]
    greeted = [(m, other) for other in near]
    greeted += [(lax.rem(m + k, MEM_COUNT), t) for k in range(1, MEM_COUNT)]
    for device in greeted:
        pl.semaphore_signal(barrier, inc=1, device_id=device, device_id_type=MESH)

    def tell():
        for n, k in enumerate((PLANE, -PLANE)):
            pl.semaphore_signal(
                known_sem.at[n], inc=1, device_id=(m, tile_at(k)), device_id_type=MESH
            )

    def hear():
        for n in range(2):
            pl.semaphore_wait(known_sem.at[n], 1)

    loads = []
    for h in range(HALVES):
        cols = pl.ds(h * LANES, LANES)
        loads.append((ctrl.at[:, cols], ctrl_nat.at[h]))
        loads.append((diff.at[:, cols], small_in.at[0, h]))
        loads.append((adv.at[:, cols], small_in.at[1, h]))
        loads.append((upw.at[:, cols], upw_in.at[h]))
    first_loads = len(loads)
    loads.append((pert, pert_half))
    for h in range(HALVES):
        cols = pl.ds(h * LANES, LANES)
        loads.append((innov.at[:, cols], obs_in.at[0, h]))
        loads.append((weight.at[:, cols], obs_in.at[1, h]))
    loads = [
        pltpu.make_async_copy(src, dst, in_sem.at[n]) for n, (src, dst) in enumerate(loads)
    ]
    for copy in loads:
        copy.start()

    lane = lax.broadcasted_iota(jnp.int32, (SUB, LANES), 1)
    sub = lax.broadcasted_iota(jnp.int32, (SUB, LANES), 0)
    low_sub = sub < SUB // 2
    at_last = lane == LANES - 1
    at_first = lane == 0

    for copy in loads[:first_loads]:
        copy.wait()

    def place_control(r, c):
        for h in range(HALVES):
            for g in range(GROUPS):
                field[r + WIDE, h, pl.ds(SUB * g, SUB), :] = ctrl_nat[
                    h, pl.ds(SUB * g * ROWS + r, SUB, stride=ROWS), :
                ]
        return c

    lax.fori_loop(0, ROWS, place_control, 0, unroll=4)
    for h in range(HALVES):
        raw[0, h, pl.ds(WIDE, ROWS), :] = small_in[0, h]
        raw[1, h, pl.ds(WIDE, ROWS), :] = small_in[1, h]
        raw[2, h, pl.ds(WIDE, ROWS), :] = jnp.where(upw_in[h] == 1, 1.0, 0.0)

    def to_neighbours(buffer, low, high, depth, first):
        copies = []
        for n, (row, shift, dest) in enumerate(
            ((low, ROWS, tile_at(-1)), (high, -ROWS, tile_at(1)))
        ):
            copies.append(
                pltpu.make_async_remote_copy(
                    src_ref=buffer(row + WIDE, depth),
                    dst_ref=buffer(row + WIDE + shift, depth),
                    send_sem=halo_send.at[first + n],
                    recv_sem=halo_recv.at[first + n],
                    device_id=(m, dest),
                    device_id_type=MESH,
                )
            )
        for copy in copies:
            copy.start()
        return copies

    def rows_of(ref):
        return lambda start, count: ref.at[pl.ds(start, count)]

    pl.semaphore_wait(barrier, len(greeted))

    ctrl_copies = to_neighbours(rows_of(field), 0, ROWS - NEAR, NEAR, 2)
    coef_copies = to_neighbours(
        lambda start, count: raw.at[:, :, pl.ds(start, count), :], 0, ROWS - WIDE, WIDE, 0
    )
    tell()

    def shifted(pair):
        lanes = lax.broadcasted_iota(jnp.int32, pair[0].shape, 1)
        right = [pltpu.roll(x, LANES - 1, 1) for x in pair]
        left = [pltpu.roll(x, 1, 1) for x in pair]
        right = [
            jnp.where(lanes == LANES - 1, right[1], right[0]),
            jnp.where(lanes == LANES - 1, 0.0, right[1]),
        ]
        left = [
            jnp.where(lanes == 0, 0.0, left[0]),
            jnp.where(lanes == 0, left[0], left[1]),
        ]
        return right, left

    top_tile = t == 0
    bottom_tile = t == TILE_COUNT - 1

    def forward_coef(block):
        rows = pl.ds(SUB * block, SUB)
        for h in range(HALVES):
            k = raw[0, h, rows, :]
            a = raw[1, h, rows, :]
            u = raw[2, h, rows, :]
            below = k + a * u
            above = k + a * (1.0 - u)
            if block == 1:
                above = jnp.where(jnp.logical_and(sub == 0, top_tile), 0.0, above)
            if block == 2:
                below = jnp.where(jnp.logical_and(sub == SUB - 1, bottom_tile), 0.0, below)
            coef[FORWARD + 0, h, rows, :] = 1.0 - 4.0 * k - a
            coef[FORWARD + 1, h, rows, :] = below
            coef[FORWARD + 2, h, rows, :] = above
            coef[FORWARD + 3, h, rows, :] = jnp.where(at_last, 0.0, k) if h else k
            coef[FORWARD + 4, h, rows, :] = k if h else jnp.where(at_first, 0.0, k)

    def adjoint_coef():
        row = lax.broadcasted_iota(jnp.int32, (EXT, LANES), 0)
        top = jnp.logical_and(row == WIDE, top_tile)
        bottom = jnp.logical_and(row == WIDE + ROWS - 1, bottom_tile)
        right, left = shifted([raw[0, h] for h in range(HALVES)])
        for h in range(HALVES):
            k = raw[0, h]
            a = raw[1, h]
            u = raw[2, h]
            below = k + a * u
            above = k + a * (1.0 - u)
            coef[ADJOINT + 0, h] = 1.0 - 4.0 * k - a
            coef[ADJOINT + 1, h] = jnp.where(bottom, 0.0, pltpu.roll(above, EXT - 1, 0))
            coef[ADJOINT + 2, h] = jnp.where(top, 0.0, pltpu.roll(below, 1, 0))
            coef[ADJOINT + 3, h] = right[h]
            coef[ADJOINT + 4, h] = left[h]

    def four_sweeps(source, target, kind, parts, add=None, together=GROUPS):
        chain = (source, level_1, level_2, level_3, target)

        def body(q, c):
            for n in range(4):
                src, dst = chain[n], chain[n + 1]
                for first, last in parts[n]:
                    for r in range(first, last):
                        f = [
                            [
                                coef[kind + i, h, pl.ds(r + WIDE, SUB, stride=0), :]
                                for h in range(HALVES)
                            ]
                            for i in range(5)
                        ]
                        for g in range(together):
                            part = pl.ds(SUB * g, SUB)
                            if together < GROUPS:
                                part = pl.ds(
                                    pl.multiple_of(SUB * (together * q + g), SUB), SUB
                                )
                            above, centre, below = [
                                [src[r + WIDE + d, h, part, :] for h in range(HALVES)]
                                for d in range(-1, 2)
                            ]
                            right = [pltpu.roll(x, LANES - 1, 1) for x in centre]
                            left = [pltpu.roll(x, 1, 1) for x in centre]
                            right = [jnp.where(at_last, right[1], right[0]), right[1]]
                            left = [left[0], jnp.where(at_first, left[0], left[1])]
                            for h in range(HALVES):
                                value = (f[0][h] * centre[h] + f[1][h] * below[h]) + (
                                    f[2][h] * above[h]
                                    + (f[3][h] * right[h] + f[4][h] * left[h])
                                )
                                if add is not None and n == 3:
                                    value = value + add[r + WIDE, h, part, :]
                                dst[r + WIDE, h, part, :] = value
            return c

        if together == GROUPS:
            body(0, 0)
        else:
            lax.fori_loop(0, GROUPS // together, body, 0)

    inner = [[(n, ROWS - n)] for n in range(1, 5)]
    near_rim = [[(n - 4, n), (ROWS - n, ROWS + 4 - n)] for n in range(1, 5)]
    wide_rim = [[(n - 8, n), (ROWS - n, ROWS + 8 - n)] for n in range(1, 5)]
    core = [[(5, 11)], [(6, 10)], [(7, 9)], []]
    core_rim = [[(n - 4, 4 + n), (12 - n, 20 - n)] for n in range(1, 4)] + [[(0, ROWS)]]

    edge_rows = (0, 1, 2, 3, 12, 13, 14, 15)
    mid_rows = (8, 9, 10, 11, 4, 5, 6, 7)

    def project(rows, out):
        for s, r in enumerate(rows):
            for h in range(HALVES):
                value = [result[r + WIDE, h, pl.ds(SUB * g, SUB), :] for g in range(GROUPS)]
                for n in range(NT):
                    total = value[0] * pert_t[n, r, h, pl.ds(0, SUB), :]
                    for g in range(1, GROUPS):
                        total = total + value[g] * pert_t[n, r, h, pl.ds(SUB * g, SUB), :]
                    out[m, HALVES * n + h, pl.ds(s, 1), :] = jnp.sum(
                        total, axis=0, keepdims=True
                    )

    def to_members(out, first):
        copies = []
        for k in range(1, MEM_COUNT):
            copies.append(
                pltpu.make_async_remote_copy(
                    src_ref=out.at[m],
                    dst_ref=out.at[m],
                    send_sem=red_send.at[first, k],
                    recv_sem=red_recv.at[first, k],
                    device_id=(lax.rem(m + k, MEM_COUNT), t),
                    device_id_type=MESH,
                )
            )
        for copy in copies:
            copy.start()
        return copies

    def wait_members(out, first):
        for k in range(1, MEM_COUNT):
            pltpu.make_async_remote_copy(
                src_ref=out.at[m],
                dst_ref=out.at[lax.rem(m + MEM_COUNT - k, MEM_COUNT)],
                send_sem=red_send.at[first, k],
                recv_sem=red_recv.at[first, k],
                device_id=(lax.rem(m + k, MEM_COUNT), t),
                device_id_type=MESH,
            ).wait_recv()

    def total_of(out, index):
        total = [out[k, index] for k in range(MEM_COUNT)]
        while len(total) > 1:
            total = [a + b for a, b in zip(total[::2], total[1::2])]
        return total[0]

    def observed(which, h, n, edge):
        upper = obs_in[which, h, pl.ds(ROWS * n, SUB), :]
        lower = obs_in[which, h, pl.ds(ROWS * n + SUB, SUB), :]
        return jnp.where(low_sub, upper, lower) if edge else jnp.where(low_sub, lower, upper)

    def pull_back(dst, block, rows):
        for s, r in enumerate(rows):
            for h in range(HALVES):
                w = [
                    mis[block, HALVES * n + h, pl.ds(s, SUB, stride=0), :] for n in range(NT)
                ]
                for g in range(GROUPS):
                    part = pl.ds(SUB * g, SUB)
                    value = w[0] * pert_t[0, r, h, part, :]
                    for n in range(1, NT):
                        value = value + w[n] * pert_t[n, r, h, part, :]
                    dst[r + WIDE, h, part, :] = value

    def place(src, dst, rows):
        for r in rows:
            for h in range(HALVES):
                for g in range(GROUPS):
                    dst[h, pl.ds(SUB * g * ROWS + r, SUB, stride=ROWS), :] = src[
                        r + WIDE, h, pl.ds(SUB * g, SUB), :
                    ]

    forward_coef(1)
    forward_coef(2)
    for copy in loads[first_loads:]:
        copy.wait()

    def widen(q, c):
        rows = pl.ds(pl.multiple_of(q * ROWS, ROWS), ROWS)
        for h in range(HALVES):
            pert_nat[h, rows, :] = pert_half[rows, pl.ds(h * LANES, LANES)].astype(jnp.float32)
        return c

    lax.fori_loop(0, NT * MEMBERS, widen, 0, unroll=8)

    def place_pert(r, c):
        for n in range(NT):
            for h in range(HALVES):
                for g in range(GROUPS):
                    pert_t[n, r, h, pl.ds(SUB * g, SUB), :] = pert_nat[
                        h, pl.ds((n * MEMBERS + SUB * g) * ROWS + r, SUB, stride=ROWS), :
                    ]
        return c

    lax.fori_loop(0, ROWS, place_pert, 0, unroll=2)

    four_sweeps(field, result, FORWARD, inner, together=2)
    project(mid_rows, mid_1)
    sent_m1 = to_members(mid_1, 1)

    for copy in coef_copies + ctrl_copies:
        copy.wait()
    forward_coef(0)
    forward_coef(3)
    four_sweeps(field, result, FORWARD, near_rim)
    project(edge_rows, edge_1)
    sent_e1 = to_members(edge_1, 0)
    hear()
    tell()
    adjoint_coef()

    def misfit(block, out):
        for n in range(NT):
            for h in range(HALVES):
                mis[block, HALVES * n + h] = observed(1, h, n, block == 0) * (
                    total_of(out, HALVES * n + h) - observed(0, h, n, block == 0)
                )

    wait_members(mid_1, 1)
    misfit(1, mid_1)
    pull_back(pulled, 1, mid_rows)
    pull_copies = to_neighbours(rows_of(pulled), NEAR, ROWS - 2 * NEAR, NEAR, 4)
    wait_members(edge_1, 0)
    misfit(0, edge_1)
    pull_back(pulled, 0, edge_rows)
    pull_copies += to_neighbours(rows_of(pulled), 0, ROWS - NEAR, NEAR, 6)
    hear()
    tell()

    four_sweeps(pulled, grad, ADJOINT, inner, add=field, together=2)
    four_sweeps(grad, result, FORWARD, core, together=2)
    for copy in pull_copies:
        copy.wait()
    four_sweeps(pulled, grad, ADJOINT, wide_rim, add=field, together=2)
    four_sweeps(grad, result, FORWARD, core_rim, together=2)
    project(edge_rows, edge_2)
    sent_e2 = to_members(edge_2, 2)
    squares = []
    for r in range(ROWS):
        for h in range(HALVES):
            for g in range(GROUPS):
                x = grad[r + WIDE, h, pl.ds(SUB * g, SUB), :]
                squares.append(x * x)
    while len(squares) > 1:
        squares = [a + b for a, b in zip(squares[::2], squares[1::2])]
    mid_2[m, NT * HALVES] = squares[0]
    project(mid_rows, mid_2)
    sent_m2 = to_members(mid_2, 3)
    hear()
    tell()
    place(grad, grad_nat, range(ROWS))
    stores = []

    def store(src, dst, first):
        for h in range(HALVES):
            copy = pltpu.make_async_copy(
                src.at[h], dst.at[:, pl.ds(h * LANES, LANES)], out_sem.at[first + h]
            )
            copy.start()
            stores.append(copy)

    store(grad_nat, grad_out, 0)

    def weigh(block, out, total):
        for n in range(NT):
            for h in range(HALVES):
                image = total_of(out, HALVES * n + h)
                weighted = observed(1, h, n, block == 0) * image
                mis[2 + block, HALVES * n + h] = weighted
                total = total + image * weighted
        return total

    wait_members(edge_2, 2)
    observed_sum = weigh(0, edge_2, jnp.zeros((SUB, LANES), jnp.float32))
    pull_back(pulled_2, 2, edge_rows)
    last_copies = to_neighbours(rows_of(pulled_2), 0, ROWS - NEAR, NEAR, 8)
    hear()
    wait_members(mid_2, 3)
    observed_sum = weigh(1, mid_2, observed_sum)
    squares = total_of(mid_2, NT * HALVES)

    scal[t] = jnp.where(
        low_sub,
        jnp.broadcast_to(jnp.sum(squares, axis=0, keepdims=True), (SUB, LANES)),
        jnp.broadcast_to(jnp.sum(observed_sum, axis=0, keepdims=True), (SUB, LANES)),
    )

    def scalar_copy(k, slot):
        return pltpu.make_async_remote_copy(
            src_ref=scal.at[t],
            dst_ref=scal.at[slot],
            send_sem=scal_send.at[k],
            recv_sem=scal_recv.at[k],
            device_id=(m, lax.rem(t + k, TILE_COUNT)),
            device_id_type=MESH,
        )

    def send_scalar(k, c):
        scalar_copy(k, t).start()
        return c

    lax.fori_loop(1, TILE_COUNT, send_scalar, 0)

    pull_back(pulled_2, 3, mid_rows)
    four_sweeps(pulled_2, result, ADJOINT, inner, add=grad, together=2)
    place(result, hess_nat, mid_rows)
    for copy in last_copies:
        copy.wait()
    four_sweeps(pulled_2, result, ADJOINT, near_rim, add=grad)
    place(result, hess_nat, edge_rows)
    store(hess_nat, hess_out, HALVES)

    def wait_scalar(k, c):
        copy = scalar_copy(k, lax.rem(t + TILE_COUNT - k, TILE_COUNT))
        copy.wait_recv()
        copy.wait_send()
        return c

    lax.fori_loop(1, TILE_COUNT, wait_scalar, 0)
    sums = [scal[k] for k in range(TILE_COUNT)]
    while len(sums) > 1:
        sums = [a + b for a, b in zip(sums[::2], sums[1::2])]
    both = jnp.sum(sums[0], axis=1, keepdims=True)
    all_squares = both[0:1]
    step_out[...] = all_squares / (all_squares + both[SUB // 2 : SUB // 2 + 1])

    for copies in (sent_e1, sent_m1, sent_e2, sent_m2):
        for copy in copies:
            copy.wait_send()
    for copy in stores:
        copy.wait()


def shards(perturbations, control, innovation, obs_weight, diffusion, advection, upwind):
    f32 = jnp.float32
    cells = MEMBERS * ROWS
    width = HALVES * LANES
    any_space = pl.BlockSpec(memory_space=pl.ANY)

    def lines(count):
        return pltpu.VMEM((count, HALVES, MEMBERS, LANES), f32)

    def sums(count):
        return pltpu.VMEM((MEM_COUNT, count, SUB, LANES), f32)

    gradient, hessian, step = pl.pallas_call(
        kernel,
        out_shape=(
            jax.ShapeDtypeStruct((cells, width), f32),
            jax.ShapeDtypeStruct((cells, width), f32),
            jax.ShapeDtypeStruct((1, 1), f32),
        ),
        in_specs=[any_space] * 7,
        out_specs=(any_space, any_space, pl.BlockSpec(memory_space=pltpu.VMEM)),
        scratch_shapes=[
            pltpu.VMEM((HALVES, cells, LANES), f32),
            pltpu.VMEM((NT * cells, width), jnp.bfloat16),
            pltpu.VMEM((HALVES, NT * cells, LANES), f32),
            pltpu.VMEM((NT, ROWS, HALVES, MEMBERS, LANES), f32),
            pltpu.VMEM((2, HALVES, ROWS, LANES), f32),
            pltpu.VMEM((HALVES, ROWS, LANES), jnp.int32),
            pltpu.VMEM((2, HALVES, NT * ROWS, LANES), f32),
            pltpu.VMEM((3, HALVES, EXT, LANES), f32),
            pltpu.VMEM((10, HALVES, EXT, LANES), f32),
            *[lines(EXT)] * 8,
            sums(NT * HALVES),
            sums(NT * HALVES),
            sums(NT * HALVES),
            sums(NT * HALVES + 1),
            pltpu.VMEM((4, NT * HALVES, SUB, LANES), f32),
            pltpu.VMEM((TILE_COUNT, SUB, LANES), f32),
            pltpu.VMEM((HALVES, cells, LANES), f32),
            pltpu.VMEM((HALVES, cells, LANES), f32),
            pltpu.SemaphoreType.DMA((13,)),
            pltpu.SemaphoreType.DMA((4,)),
            pltpu.SemaphoreType.DMA((10,)),
            pltpu.SemaphoreType.DMA((10,)),
            pltpu.SemaphoreType.DMA((4, MEM_COUNT)),
            pltpu.SemaphoreType.DMA((4, MEM_COUNT)),
            pltpu.SemaphoreType.DMA((TILE_COUNT,)),
            pltpu.SemaphoreType.DMA((TILE_COUNT,)),
            pltpu.SemaphoreType.REGULAR((2,)),
        ],
        compiler_params=pltpu.CompilerParams(
            collective_id=0, has_side_effects=True, vmem_limit_bytes=63 << 20
        ),
    )(
        control.reshape(cells, width),
        perturbations.reshape(NT * cells, width),
        innovation.reshape(NT * ROWS, width),
        obs_weight.reshape(NT * ROWS, width),
        diffusion,
        advection,
        upwind,
    )
    return (
        gradient.reshape(control.shape),
        hessian.reshape(control.shape),
        step.reshape(()),
    )


def solution(mesh):
    return jax.shard_map(
        shards,
        mesh=mesh,
        in_specs=(
            P(None, "mem", "tile", None),
            P("mem", "tile", None),
            P(None, "tile", None),
            P(None, "tile", None),
            P("tile", None),
            P("tile", None),
            P("tile", None),
        ),
        out_specs=(P("mem", "tile", None), P("mem", "tile", None), P()),
        check_vma=False,
    )
```

time: 68.8 us -> 51.9 us (0.75)
  Pallas kernels: 63.6 us -> 46.4 us
    pallas_call x1, Pallas kernels: 63.6 us -> 46.4 us  [shards(): pl.pallas_call(kernel, out_shape=(jax.ShapeDtypeStruct((cells, width), f3...]
where the time goes in v2:
time: 51.9 us; the launch traced here: 51.5 us
  Pallas kernels  46.4 us (89%)
  local copies, waits for them, and re-layouts  2.72 us (5%)
  between operations  2.41 us (5%)
    pallas_call x1, Pallas kernels, shards(): pl.pallas_call(kernel, out_shape=(jax.ShapeDtypeStruct((cells, width), f3...  46.4 us
    unnamed x4, local copies, waits for them, and re-layouts  2.72 us

profile of v2, /device:TPU:1, one launch (start us, length us, event | category | flops | bytes accessed | tf_op | source)
XLA Modules:
  0.0 51.5 jit_solution(12436694145102345757)
XLA Ops:
  0.6 46.4 %shard_map.94 = (f32[512,256]{1,0:T(8,128)}, f32[512,256]{1,0:T(8,128)}, f32[1,1]{1,0:T(1,128)}) custom-call(f32[512,256]{1,0:T(8,128)} %bitcast.10, bf16[1536,256]{1,0:T(8,128)(2,1)} %bitcast.7, f32[48,256]{1,0:T(8,128)} %bitcast.11, f32[48,256]{1,0:T(8,128)} %bitcast.12, f32[16,256]{1,0:T(8,128)} %diff.1, f32[16,256]{1,0:T(8,128)} %adv.1, s32[16,256]{1,0:T(8,128)} %upw.1), custom_call_target="tpu_custom_call" | custom-call | tf_op jit(solution)/shard_map/pallas_call | solution.py:520
  47.0 0.0 copy-start
  47.0 1.9 %copy.13 = f32[32,16,256]{2,1,0:T(8,128)} copy(f32[32,16,256]{2,1,0:T(8,128)} %bitcast.9) | data formatting | bytes 1048576
  49.0 0.0 copy-done
  49.0 0.8 %copy.14 = f32[32,16,256]{2,1,0:T(8,128)} copy(f32[32,16,256]{2,1,0:T(8,128)S(1)} %bitcast.8) | data formatting | bytes 1048576
Async XLA Ops:
  47.0 1.9 %copy-start = (f32[512,256]{1,0:T(8,128)S(1)}, f32[512,256]{1,0:T(8,128)}, u32[]{:S(2)}) copy-start(f32[512,256]{1,0:T(8,128)} %get-tuple-element.7) | copy-start | bytes 1572868

commit v3 on v2

--- a/solution.py
+++ b/solution.py
@@ -15,6 +15,7 @@
 ROWS = 16
 MEMBERS = 32
 GROUPS = MEMBERS // SUB
+HALF = MEMBERS // 2
 MEM_COUNT = 8
 TILE_COUNT = 32
 WIDE = 8
@@ -137,6 +138,10 @@
         raw[1, h, pl.ds(WIDE, ROWS), :] = small_in[1, h]
         raw[2, h, pl.ds(WIDE, ROWS), :] = jnp.where(upw_in[h] == 1, 1.0, 0.0)
 
+    def half_rows(ref, half):
+        part = pl.ds(HALF * half, HALF)
+        return lambda start, count: ref.at[pl.ds(start, count), :, part, :]
+
     def to_neighbours(buffer, low, high, depth, first):
         copies = []
         for n, (row, shift, dest) in enumerate(
@@ -156,15 +161,14 @@
             copy.start()
         return copies
 
-    def rows_of(ref):
-        return lambda start, count: ref.at[pl.ds(start, count)]
-
     pl.semaphore_wait(barrier, len(greeted))
 
-    ctrl_copies = to_neighbours(rows_of(field), 0, ROWS - NEAR, NEAR, 2)
     coef_copies = to_neighbours(
         lambda start, count: raw.at[:, :, pl.ds(start, count), :], 0, ROWS - WIDE, WIDE, 0
     )
+    ctrl_copies = [
+        to_neighbours(half_rows(field, q), 0, ROWS - NEAR, NEAR, 2 + 2 * q) for q in range(2)
+    ]
     tell()
 
     def shifted(pair):
@@ -219,8 +223,9 @@
             coef[ADJOINT + 3, h] = right[h]
             coef[ADJOINT + 4, h] = left[h]
 
-    def four_sweeps(source, target, kind, parts, add=None, together=GROUPS):
+    def four_sweeps(source, target, kind, parts, add=None, only=None):
         chain = (source, level_1, level_2, level_3, target)
+        together = GROUPS // 2
 
         def body(q, c):
             for n in range(4):
@@ -235,11 +240,10 @@
                             for i in range(5)
                         ]
                         for g in range(together):
-                            part = pl.ds(SUB * g, SUB)
-                            if together < GROUPS:
-                                part = pl.ds(
-                                    pl.multiple_of(SUB * (together * q + g), SUB), SUB
-                                )
+                            part = SUB * (together * q + g)
+                            part = pl.ds(
+                                part if only is not None else pl.multiple_of(part, SUB), SUB
+                            )
                             above, centre, below = [
                                 [src[r + WIDE + d, h, part, :] for h in range(HALVES)]
                                 for d in range(-1, 2)
@@ -258,19 +262,21 @@
                                 dst[r + WIDE, h, part, :] = value
             return c
 
-        if together == GROUPS:
-            body(0, 0)
+        if only is not None:
+            body(only, 0)
         else:
-            lax.fori_loop(0, GROUPS // together, body, 0)
+            lax.fori_loop(0, 2, body, 0)
 
     inner = [[(n, ROWS - n)] for n in range(1, 5)]
     near_rim = [[(n - 4, n), (ROWS - n, ROWS + 4 - n)] for n in range(1, 5)]
     wide_rim = [[(n - 8, n), (ROWS - n, ROWS + 8 - n)] for n in range(1, 5)]
     core = [[(5, 11)], [(6, 10)], [(7, 9)], []]
-    core_rim = [[(n - 4, 4 + n), (12 - n, 20 - n)] for n in range(1, 4)] + [[(0, ROWS)]]
+    core_edge = [[(-3, 5), (11, 19)], [(-2, 6), (10, 18)], [(-1, 5), (11, 17)], [(0, 4), (12, 16)]]
+    core_mid = [[], [], [(5, 7), (9, 11)], [(4, 12)]]
 
     edge_rows = (0, 1, 2, 3, 12, 13, 14, 15)
     mid_rows = (8, 9, 10, 11, 4, 5, 6, 7)
+    group_half = ((0, 1), (2, 3))
 
     def project(rows, out):
         for s, r in enumerate(rows):
@@ -323,13 +329,13 @@
         lower = obs_in[which, h, pl.ds(ROWS * n + SUB, SUB), :]
         return jnp.where(low_sub, upper, lower) if edge else jnp.where(low_sub, lower, upper)
 
-    def pull_back(dst, block, rows):
+    def pull_back(dst, block, rows, groups=range(GROUPS)):
         for s, r in enumerate(rows):
             for h in range(HALVES):
                 w = [
                     mis[block, HALVES * n + h, pl.ds(s, SUB, stride=0), :] for n in range(NT)
                 ]
-                for g in range(GROUPS):
+                for g in groups:
                     part = pl.ds(SUB * g, SUB)
                     value = w[0] * pert_t[0, r, h, part, :]
                     for n in range(1, NT):
@@ -368,15 +374,20 @@
 
     lax.fori_loop(0, ROWS, place_pert, 0, unroll=2)
 
-    four_sweeps(field, result, FORWARD, inner, together=2)
+    four_sweeps(field, result, FORWARD, inner)
     project(mid_rows, mid_1)
     sent_m1 = to_members(mid_1, 1)
-
-    for copy in coef_copies + ctrl_copies:
+    hear()
+    tell()
+
+    for copy in coef_copies:
         copy.wait()
     forward_coef(0)
     forward_coef(3)
-    four_sweeps(field, result, FORWARD, near_rim)
+    for q in range(2):
+        for copy in ctrl_copies[q]:
+            copy.wait()
+        four_sweeps(field, result, FORWARD, near_rim, only=q)
     project(edge_rows, edge_1)
     sent_e1 = to_members(edge_1, 0)
     hear()
@@ -393,35 +404,46 @@
     wait_members(mid_1, 1)
     misfit(1, mid_1)
     pull_back(pulled, 1, mid_rows)
-    pull_copies = to_neighbours(rows_of(pulled), NEAR, ROWS - 2 * NEAR, NEAR, 4)
+    pull_copies = [
+        to_neighbours(half_rows(pulled, q), NEAR, ROWS - 2 * NEAR, NEAR, 6 + 2 * q)
+        for q in range(2)
+    ]
+    hear()
+    tell()
     wait_members(edge_1, 0)
     misfit(0, edge_1)
-    pull_back(pulled, 0, edge_rows)
-    pull_copies += to_neighbours(rows_of(pulled), 0, ROWS - NEAR, NEAR, 6)
+    for q in range(2):
+        pull_back(pulled, 0, edge_rows, group_half[q])
+        pull_copies[q] += to_neighbours(
+            half_rows(pulled, q), 0, ROWS - NEAR, NEAR, 10 + 2 * q
+        )
+
+    def square(rows):
+        squares = []
+        for r in rows:
+            for h in range(HALVES):
+                for g in range(GROUPS):
+                    x = grad[r + WIDE, h, pl.ds(SUB * g, SUB), :]
+                    squares.append(x * x)
+        while len(squares) > 1:
+            squares = [a + b for a, b in zip(squares[::2], squares[1::2])]
+        return squares[0]
+
+    four_sweeps(pulled, grad, ADJOINT, inner, add=field)
+    four_sweeps(grad, result, FORWARD, core)
+    mid_2[m, NT * HALVES] = square(mid_rows)
     hear()
-    tell()
-
-    four_sweeps(pulled, grad, ADJOINT, inner, add=field, together=2)
-    four_sweeps(grad, result, FORWARD, core, together=2)
-    for copy in pull_copies:
-        copy.wait()
-    four_sweeps(pulled, grad, ADJOINT, wide_rim, add=field, together=2)
-    four_sweeps(grad, result, FORWARD, core_rim, together=2)
+    for q in range(2):
+        for copy in pull_copies[q]:
+            copy.wait()
+        four_sweeps(pulled, grad, ADJOINT, wide_rim, add=field, only=q)
+        four_sweeps(grad, result, FORWARD, core_edge, only=q)
     project(edge_rows, edge_2)
     sent_e2 = to_members(edge_2, 2)
-    squares = []
-    for r in range(ROWS):
-        for h in range(HALVES):
-            for g in range(GROUPS):
-                x = grad[r + WIDE, h, pl.ds(SUB * g, SUB), :]
-                squares.append(x * x)
-    while len(squares) > 1:
-        squares = [a + b for a, b in zip(squares[::2], squares[1::2])]
-    mid_2[m, NT * HALVES] = squares[0]
+    mid_2[m, NT * HALVES] += square(edge_rows)
+    four_sweeps(grad, result, FORWARD, core_mid)
     project(mid_rows, mid_2)
     sent_m2 = to_members(mid_2, 3)
-    hear()
-    tell()
     place(grad, grad_nat, range(ROWS))
     stores = []
 
@@ -446,26 +468,32 @@
 
     wait_members(edge_2, 2)
     observed_sum = weigh(0, edge_2, jnp.zeros((SUB, LANES), jnp.float32))
-    pull_back(pulled_2, 2, edge_rows)
-    last_copies = to_neighbours(rows_of(pulled_2), 0, ROWS - NEAR, NEAR, 8)
-    hear()
+    last_copies = []
+    for q in range(2):
+        pull_back(pulled_2, 2, edge_rows, group_half[q])
+        last_copies.append(
+            to_neighbours(half_rows(pulled_2, q), 0, ROWS - NEAR, NEAR, 14 + 2 * q)
+        )
     wait_members(mid_2, 3)
     observed_sum = weigh(1, mid_2, observed_sum)
     squares = total_of(mid_2, NT * HALVES)
 
-    scal[t] = jnp.where(
-        low_sub,
-        jnp.broadcast_to(jnp.sum(squares, axis=0, keepdims=True), (SUB, LANES)),
-        jnp.broadcast_to(jnp.sum(observed_sum, axis=0, keepdims=True), (SUB, LANES)),
-    )
+    def fold(x):
+        x = jnp.sum(x, axis=0, keepdims=True)
+        return x + pltpu.roll(x, LANES // 2, 1)
+
+    low_lane = lax.broadcasted_iota(jnp.int32, (1, LANES), 1) < LANES // 2
+    scal[t] = jnp.where(low_lane, fold(squares), fold(observed_sum))
 
     def scalar_copy(k, slot):
+        dest = lax.rem(t + k, TILE_COUNT)
+        side = lax.rem(t // 2 + dest // 2, 2)
         return pltpu.make_async_remote_copy(
             src_ref=scal.at[t],
             dst_ref=scal.at[slot],
             send_sem=scal_send.at[k],
             recv_sem=scal_recv.at[k],
-            device_id=(m, lax.rem(t + k, TILE_COUNT)),
+            device_id=(lax.rem(m + side * (MEM_COUNT // 2), MEM_COUNT), dest),
             device_id_type=MESH,
         )
 
@@ -476,11 +504,12 @@
     lax.fori_loop(1, TILE_COUNT, send_scalar, 0)
 
     pull_back(pulled_2, 3, mid_rows)
-    four_sweeps(pulled_2, result, ADJOINT, inner, add=grad, together=2)
+    four_sweeps(pulled_2, result, ADJOINT, inner, add=grad)
     place(result, hess_nat, mid_rows)
-    for copy in last_copies:
-        copy.wait()
-    four_sweeps(pulled_2, result, ADJOINT, near_rim, add=grad)
+    for q in range(2):
+        for copy in last_copies[q]:
+            copy.wait()
+        four_sweeps(pulled_2, result, ADJOINT, near_rim, add=grad, only=q)
     place(result, hess_nat, edge_rows)
     store(hess_nat, hess_out, HALVES)
 
@@ -494,14 +523,28 @@
     sums = [scal[k] for k in range(TILE_COUNT)]
     while len(sums) > 1:
         sums = [a + b for a, b in zip(sums[::2], sums[1::2])]
-    both = jnp.sum(sums[0], axis=1, keepdims=True)
-    all_squares = both[0:1]
-    step_out[...] = all_squares / (all_squares + both[SUB // 2 : SUB // 2 + 1])
+    all_squares = jnp.sum(jnp.where(low_lane, sums[0], 0.0), axis=1, keepdims=True)
+    all_observed = jnp.sum(jnp.where(low_lane, 0.0, sums[0]), axis=1, keepdims=True)
+    step_out[...] = all_squares / (all_squares + all_observed)
 
     for copies in (sent_e1, sent_m1, sent_e2, sent_m2):
         for copy in copies:
             copy.wait_send()
     for copy in stores:
+        copy.wait()
+
+
+def hand_over(grad_in, hess_in, grad_out, hess_out, sem):
+    pieces = sem.shape[1]
+    copies = []
+    for n, (src, dst) in enumerate(((grad_in, grad_out), (hess_in, hess_out))):
+        rows = src.shape[0] // pieces
+        for k in range(pieces):
+            part = pl.ds(rows * k, rows)
+            copies.append(pltpu.make_async_copy(src.at[part], dst.at[part], sem.at[n, k]))
+    for copy in copies:
+        copy.start()
+    for copy in copies:
         copy.wait()
 
 
@@ -542,13 +585,13 @@
             sums(NT * HALVES),
             sums(NT * HALVES + 1),
             pltpu.VMEM((4, NT * HALVES, SUB, LANES), f32),
-            pltpu.VMEM((TILE_COUNT, SUB, LANES), f32),
+            pltpu.VMEM((TILE_COUNT, 1, LANES), f32),
             pltpu.VMEM((HALVES, cells, LANES), f32),
             pltpu.VMEM((HALVES, cells, LANES), f32),
             pltpu.SemaphoreType.DMA((13,)),
             pltpu.SemaphoreType.DMA((4,)),
-            pltpu.SemaphoreType.DMA((10,)),
-            pltpu.SemaphoreType.DMA((10,)),
+            pltpu.SemaphoreType.DMA((18,)),
+            pltpu.SemaphoreType.DMA((18,)),
             pltpu.SemaphoreType.DMA((4, MEM_COUNT)),
             pltpu.SemaphoreType.DMA((4, MEM_COUNT)),
             pltpu.SemaphoreType.DMA((TILE_COUNT,)),
@@ -567,6 +610,13 @@
         advection,
         upwind,
     )
+    gradient, hessian = pl.pallas_call(
+        hand_over,
+        out_shape=(jax.ShapeDtypeStruct((cells, width), f32),) * 2,
+        in_specs=[any_space] * 2,
+        out_specs=(any_space, any_space),
+        scratch_shapes=[pltpu.SemaphoreType.DMA((2, 4))],
+    )(gradient, hessian)
     return (
         gradient.reshape(control.shape),
         hessian.reshape(control.shape),

time: 51.9 us -> 79.1 us (1.52)
  Pallas kernels: 46.4 us -> 76.6 us
  local copies, waits for them, and re-layouts: 2.72 us -> 0 us
    pallas_call x0 -> x1, Pallas kernels: none -> 32.9 us  [shards(): pl.pallas_call(hand_over, out_shape=(jax.ShapeDtypeStruct((cells, width),...]
    pallas_call x1, Pallas kernels: 46.4 us -> 43.6 us  [shards(): pl.pallas_call(kernel, out_shape=(jax.ShapeDtypeStruct((cells, width), f3...]
    unnamed x4 -> x0, local copies, waits for them, and re-layouts: 2.72 us -> none
where the time goes in v3:
time: 79.1 us; the launch traced here: 79 us
  Pallas kernels  76.6 us (97%)
  between operations  2.4 us (3%)
    pallas_call x1, Pallas kernels, shards(): pl.pallas_call(kernel, out_shape=(jax.ShapeDtypeStruct((cells, width), f3...  43.6 us
    pallas_call x1, Pallas kernels, shards(): pl.pallas_call(hand_over, out_shape=(jax.ShapeDtypeStruct((cells, width),...  32.9 us

profile of v3, /device:TPU:1, one launch (start us, length us, event | category | flops | bytes accessed | tf_op | source)
XLA Modules:
  0.0 79.0 jit_solution(16779395671462806306)
XLA Ops:
  0.6 43.6 %shard_map.94 = (f32[512,256]{1,0:T(8,128)}, f32[512,256]{1,0:T(8,128)}, f32[1,1]{1,0:T(1,128)}) custom-call(f32[512,256]{1,0:T(8,128)} %bitcast.8, bf16[1536,256]{1,0:T(8,128)(2,1)} %bitcast.7, f32[48,256]{1,0:T(8,128)} %bitcast.9, f32[48,256]{1,0:T(8,128)} %bitcast.10, f32[16,256]{1,0:T(8,128)} %diff.1, f32[16,256]{1,0:T(8,128)} %adv.1, s32[16,256]{1,0:T(8,128)} %upw.1), custom_call_target="tpu_custom_call" | custom-call | tf_op jit(solution)/shard_map/pallas_call | solution.py:563
  44.3 32.9 %shard_map.95 = (f32[512,256]{1,0:T(8,128)}, f32[512,256]{1,0:T(8,128)}) custom-call(f32[512,256]{1,0:T(8,128)} %get-tuple-element.8.grad_in, f32[512,256]{1,0:T(8,128)} %get-tuple-element.9.hess_in), custom_call_target="tpu_custom_call" | custom-call | tf_op jit(solution)/shard_map/pallas_call | solution.py:613

commit v4 on v3

--- a/solution.py
+++ b/solution.py
@@ -138,37 +138,58 @@
         raw[1, h, pl.ds(WIDE, ROWS), :] = small_in[1, h]
         raw[2, h, pl.ds(WIDE, ROWS), :] = jnp.where(upw_in[h] == 1, 1.0, 0.0)
 
-    def half_rows(ref, half):
-        part = pl.ds(HALF * half, HALF)
-        return lambda start, count: ref.at[pl.ds(start, count), :, part, :]
-
-    def to_neighbours(buffer, low, high, depth, first):
-        copies = []
-        for n, (row, shift, dest) in enumerate(
-            ((low, ROWS, tile_at(-1)), (high, -ROWS, tile_at(1)))
-        ):
-            copies.append(
-                pltpu.make_async_remote_copy(
-                    src_ref=buffer(row + WIDE, depth),
-                    dst_ref=buffer(row + WIDE + shift, depth),
-                    send_sem=halo_send.at[first + n],
-                    recv_sem=halo_recv.at[first + n],
-                    device_id=(m, dest),
-                    device_id_type=MESH,
-                )
+    def neighbour_copies(buffer, low, high, depth, first):
+        return [
+            pltpu.make_async_remote_copy(
+                src_ref=buffer(row + WIDE, depth),
+                dst_ref=buffer(row + WIDE + shift, depth),
+                send_sem=halo_send.at[first + n],
+                recv_sem=halo_recv.at[first + n],
+                device_id=(m, dest),
+                device_id_type=MESH,
             )
+            for n, (row, shift, dest) in enumerate(
+                ((low, ROWS, tile_at(-1)), (high, -ROWS, tile_at(1)))
+            )
+        ]
+
+    def half_copies(ref, low, high, depth, first, q):
+        part = pl.ds(pl.multiple_of(HALF * q, HALF), HALF)
+        return neighbour_copies(
+            lambda start, count: ref.at[pl.ds(start, count), :, part, :],
+            low,
+            high,
+            depth,
+            first + 2 * q,
+        )
+
+    def start_all(copies):
         for copy in copies:
             copy.start()
-        return copies
+
+    def wait_all(copies):
+        for copy in copies:
+            copy.wait()
+
+    def each_half(step):
+        def body(q, c):
+            step(q)
+            return c
+
+        lax.fori_loop(0, 2, body, 0)
+
+    ctrl_halo = functools.partial(half_copies, field, 0, ROWS - NEAR, NEAR, 2)
+    pull_halo_mid = functools.partial(half_copies, pulled, NEAR, ROWS - 2 * NEAR, NEAR, 6)
+    pull_halo_edge = functools.partial(half_copies, pulled, 0, ROWS - NEAR, NEAR, 10)
+    last_halo = functools.partial(half_copies, pulled_2, 0, ROWS - NEAR, NEAR, 14)
 
     pl.semaphore_wait(barrier, len(greeted))
 
-    coef_copies = to_neighbours(
+    coef_copies = neighbour_copies(
         lambda start, count: raw.at[:, :, pl.ds(start, count), :], 0, ROWS - WIDE, WIDE, 0
     )
-    ctrl_copies = [
-        to_neighbours(half_rows(field, q), 0, ROWS - NEAR, NEAR, 2 + 2 * q) for q in range(2)
-    ]
+    start_all(coef_copies)
+    each_half(lambda q: start_all(ctrl_halo(q)))
     tell()
 
     def shifted(pair):
@@ -223,7 +244,7 @@
             coef[ADJOINT + 3, h] = right[h]
             coef[ADJOINT + 4, h] = left[h]
 
-    def four_sweeps(source, target, kind, parts, add=None, only=None):
+    def four_sweeps(source, target, kind, parts, add=None, half=None):
         chain = (source, level_1, level_2, level_3, target)
         together = GROUPS // 2
 
@@ -240,10 +261,7 @@
                             for i in range(5)
                         ]
                         for g in range(together):
-                            part = SUB * (together * q + g)
-                            part = pl.ds(
-                                part if only is not None else pl.multiple_of(part, SUB), SUB
-                            )
+                            part = pl.ds(pl.multiple_of(SUB * (together * q + g), SUB), SUB)
                             above, centre, below = [
                                 [src[r + WIDE + d, h, part, :] for h in range(HALVES)]
                                 for d in range(-1, 2)
@@ -262,8 +280,8 @@
                                 dst[r + WIDE, h, part, :] = value
             return c
 
-        if only is not None:
-            body(only, 0)
+        if half is not None:
+            body(half, 0)
         else:
             lax.fori_loop(0, 2, body, 0)
 
@@ -276,7 +294,6 @@
 
     edge_rows = (0, 1, 2, 3, 12, 13, 14, 15)
     mid_rows = (8, 9, 10, 11, 4, 5, 6, 7)
-    group_half = ((0, 1), (2, 3))
 
     def project(rows, out):
         for s, r in enumerate(rows):
@@ -329,14 +346,14 @@
         lower = obs_in[which, h, pl.ds(ROWS * n + SUB, SUB), :]
         return jnp.where(low_sub, upper, lower) if edge else jnp.where(low_sub, lower, upper)
 
-    def pull_back(dst, block, rows, groups=range(GROUPS)):
+    def pull_back(dst, block, rows, half):
         for s, r in enumerate(rows):
             for h in range(HALVES):
                 w = [
                     mis[block, HALVES * n + h, pl.ds(s, SUB, stride=0), :] for n in range(NT)
                 ]
-                for g in groups:
-                    part = pl.ds(SUB * g, SUB)
+                for g in range(GROUPS // 2):
+                    part = pl.ds(pl.multiple_of(HALF * half + SUB * g, SUB), SUB)
                     value = w[0] * pert_t[0, r, h, part, :]
                     for n in range(1, NT):
                         value = value + w[n] * pert_t[n, r, h, part, :]
@@ -380,14 +397,15 @@
     hear()
     tell()
 
-    for copy in coef_copies:
-        copy.wait()
+    wait_all(coef_copies)
     forward_coef(0)
     forward_coef(3)
-    for q in range(2):
-        for copy in ctrl_copies[q]:
-            copy.wait()
-        four_sweeps(field, result, FORWARD, near_rim, only=q)
+
+    def increment_rim(q):
+        wait_all(ctrl_halo(q))
+        four_sweeps(field, result, FORWARD, near_rim, half=q)
+
+    each_half(increment_rim)
     project(edge_rows, edge_1)
     sent_e1 = to_members(edge_1, 0)
     hear()
@@ -403,20 +421,22 @@
 
     wait_members(mid_1, 1)
     misfit(1, mid_1)
-    pull_back(pulled, 1, mid_rows)
-    pull_copies = [
-        to_neighbours(half_rows(pulled, q), NEAR, ROWS - 2 * NEAR, NEAR, 6 + 2 * q)
-        for q in range(2)
-    ]
+
+    def pull_mid(q):
+        pull_back(pulled, 1, mid_rows, q)
+        start_all(pull_halo_mid(q))
+
+    each_half(pull_mid)
     hear()
     tell()
     wait_members(edge_1, 0)
     misfit(0, edge_1)
-    for q in range(2):
-        pull_back(pulled, 0, edge_rows, group_half[q])
-        pull_copies[q] += to_neighbours(
-            half_rows(pulled, q), 0, ROWS - NEAR, NEAR, 10 + 2 * q
-        )
+
+    def pull_edge(q):
+        pull_back(pulled, 0, edge_rows, q)
+        start_all(pull_halo_edge(q))
+
+    each_half(pull_edge)
 
     def square(rows):
         squares = []
@@ -433,11 +453,13 @@
     four_sweeps(grad, result, FORWARD, core)
     mid_2[m, NT * HALVES] = square(mid_rows)
     hear()
-    for q in range(2):
-        for copy in pull_copies[q]:
-            copy.wait()
-        four_sweeps(pulled, grad, ADJOINT, wide_rim, add=field, only=q)
-        four_sweeps(grad, result, FORWARD, core_edge, only=q)
+
+    def gradient_rim(q):
+        wait_all(pull_halo_mid(q) + pull_halo_edge(q))
+        four_sweeps(pulled, grad, ADJOINT, wide_rim, add=field, half=q)
+        four_sweeps(grad, result, FORWARD, core_edge, half=q)
+
+    each_half(gradient_rim)
     project(edge_rows, edge_2)
     sent_e2 = to_members(edge_2, 2)
     mid_2[m, NT * HALVES] += square(edge_rows)
@@ -468,12 +490,12 @@
 
     wait_members(edge_2, 2)
     observed_sum = weigh(0, edge_2, jnp.zeros((SUB, LANES), jnp.float32))
-    last_copies = []
-    for q in range(2):
-        pull_back(pulled_2, 2, edge_rows, group_half[q])
-        last_copies.append(
-            to_neighbours(half_rows(pulled_2, q), 0, ROWS - NEAR, NEAR, 14 + 2 * q)
-        )
+
+    def last_edge(q):
+        pull_back(pulled_2, 2, edge_rows, q)
+        start_all(last_halo(q))
+
+    each_half(last_edge)
     wait_members(mid_2, 3)
     observed_sum = weigh(1, mid_2, observed_sum)
     squares = total_of(mid_2, NT * HALVES)
@@ -491,8 +513,8 @@
         return pltpu.make_async_remote_copy(
             src_ref=scal.at[t],
             dst_ref=scal.at[slot],
-            send_sem=scal_send.at[k],
-            recv_sem=scal_recv.at[k],
+            send_sem=scal_send,
+            recv_sem=scal_recv,
             device_id=(lax.rem(m + side * (MEM_COUNT // 2), MEM_COUNT), dest),
             device_id_type=MESH,
         )
@@ -503,23 +525,27 @@
 
     lax.fori_loop(1, TILE_COUNT, send_scalar, 0)
 
-    pull_back(pulled_2, 3, mid_rows)
+    each_half(lambda q: pull_back(pulled_2, 3, mid_rows, q))
     four_sweeps(pulled_2, result, ADJOINT, inner, add=grad)
     place(result, hess_nat, mid_rows)
-    for q in range(2):
-        for copy in last_copies[q]:
-            copy.wait()
-        four_sweeps(pulled_2, result, ADJOINT, near_rim, add=grad, only=q)
+
+    def hessian_rim(q):
+        wait_all(last_halo(q))
+        four_sweeps(pulled_2, result, ADJOINT, near_rim, add=grad, half=q)
+
+    each_half(hessian_rim)
     place(result, hess_nat, edge_rows)
     store(hess_nat, hess_out, HALVES)
 
-    def wait_scalar(k, c):
-        copy = scalar_copy(k, lax.rem(t + TILE_COUNT - k, TILE_COUNT))
-        copy.wait_recv()
-        copy.wait_send()
-        return c
-
-    lax.fori_loop(1, TILE_COUNT, wait_scalar, 0)
+    others = scal.at[pl.ds(0, TILE_COUNT - 1)]
+    pltpu.make_async_remote_copy(
+        src_ref=others,
+        dst_ref=others,
+        send_sem=scal_send,
+        recv_sem=scal_recv,
+        device_id=(m, tile_at(1)),
+        device_id_type=MESH,
+    ).wait()
     sums = [scal[k] for k in range(TILE_COUNT)]
     while len(sums) > 1:
         sums = [a + b for a, b in zip(sums[::2], sums[1::2])]
@@ -535,13 +561,9 @@
 
 
 def hand_over(grad_in, hess_in, grad_out, hess_out, sem):
-    pieces = sem.shape[1]
     copies = []
     for n, (src, dst) in enumerate(((grad_in, grad_out), (hess_in, hess_out))):
-        rows = src.shape[0] // pieces
-        for k in range(pieces):
-            part = pl.ds(rows * k, rows)
-            copies.append(pltpu.make_async_copy(src.at[part], dst.at[part], sem.at[n, k]))
+        copies.append(pltpu.make_async_copy(src, dst, sem.at[n]))
     for copy in copies:
         copy.start()
     for copy in copies:
@@ -559,6 +581,9 @@
 
     def sums(count):
         return pltpu.VMEM((MEM_COUNT, count, SUB, LANES), f32)
+
+    def pin(x):
+        return pltpu.with_memory_space_constraint(x, pltpu.HBM)
 
     gradient, hessian, step = pl.pallas_call(
         kernel,
@@ -594,28 +619,28 @@
             pltpu.SemaphoreType.DMA((18,)),
             pltpu.SemaphoreType.DMA((4, MEM_COUNT)),
             pltpu.SemaphoreType.DMA((4, MEM_COUNT)),
-            pltpu.SemaphoreType.DMA((TILE_COUNT,)),
-            pltpu.SemaphoreType.DMA((TILE_COUNT,)),
+            pltpu.SemaphoreType.DMA,
+            pltpu.SemaphoreType.DMA,
             pltpu.SemaphoreType.REGULAR((2,)),
         ],
         compiler_params=pltpu.CompilerParams(
-            collective_id=0, has_side_effects=True, vmem_limit_bytes=63 << 20
+            collective_id=0, has_side_effects=True, vmem_limit_bytes=20 << 20
         ),
     )(
-        control.reshape(cells, width),
-        perturbations.reshape(NT * cells, width),
-        innovation.reshape(NT * ROWS, width),
-        obs_weight.reshape(NT * ROWS, width),
-        diffusion,
-        advection,
-        upwind,
+        pin(control.reshape(cells, width)),
+        pin(perturbations.reshape(NT * cells, width)),
+        pin(innovation.reshape(NT * ROWS, width)),
+        pin(obs_weight.reshape(NT * ROWS, width)),
+        pin(diffusion),
+        pin(advection),
+        pin(upwind),
     )
     gradient, hessian = pl.pallas_call(
         hand_over,
         out_shape=(jax.ShapeDtypeStruct((cells, width), f32),) * 2,
         in_specs=[any_space] * 2,
         out_specs=(any_space, any_space),
-        scratch_shapes=[pltpu.SemaphoreType.DMA((2, 4))],
+        scratch_shapes=[pltpu.SemaphoreType.DMA((2,))], compiler_params=pltpu.CompilerParams(vmem_limit_bytes=1 << 20),
     )(gradient, hessian)
     return (
         gradient.reshape(control.shape),

time: 79.1 us -> 46.5 us (0.59)
  Pallas kernels: 76.6 us -> 43.7 us
    pallas_call x1, Pallas kernels: 32.9 us -> 0.99 us  [shards(): pl.pallas_call(hand_over, out_shape=(jax.ShapeDtypeStruct((cells, width),...]
    pallas_call x1, Pallas kernels: 43.6 us -> 42.7 us  [shards(): pl.pallas_call(kernel, out_shape=(jax.ShapeDtypeStruct((cells, width), f3...]
where the time goes in v4:
time: 46.5 us; the launch traced here: 46.1 us
  Pallas kernels  43.7 us (94%)
  between operations  2.41 us (5%)
    pallas_call x1, Pallas kernels, shards(): pl.pallas_call(kernel, out_shape=(jax.ShapeDtypeStruct((cells, width), f3...  42.7 us
    pallas_call x1, Pallas kernels, shards(): pl.pallas_call(hand_over, out_shape=(jax.ShapeDtypeStruct((cells, width),...  0.99 us

profile of v4, /device:TPU:1, one launch (start us, length us, event | category | flops | bytes accessed | tf_op | source)
XLA Modules:
  0.0 46.1 jit_solution(5699742148851985307)
XLA Ops:
  0.6 42.7 %shard_map.94 = (f32[512,256]{1,0:T(8,128)S(1)}, f32[512,256]{1,0:T(8,128)S(1)}, f32[1,1]{1,0:T(1,128)}) custom-call(f32[512,256]{1,0:T(8,128)} %bitcast.8, bf16[1536,256]{1,0:T(8,128)(2,1)} %bitcast.7, f32[48,256]{1,0:T(8,128)} %bitcast.9, f32[48,256]{1,0:T(8,128)} %bitcast.10, f32[16,256]{1,0:T(8,128)} %diff.1, f32[16,256]{1,0:T(8,128)} %adv.1, s32[16,256]{1,0:T(8,128)} %upw.1), custom_call_target="tpu_custom_call" | custom-call | tf_op jit(solution)/shard_map/pallas_call | solution.py:588
  43.3 1.0 %shard_map.95 = (f32[512,256]{1,0:T(8,128)}, f32[512,256]{1,0:T(8,128)}) custom-call(f32[512,256]{1,0:T(8,128)S(1)} %get-tuple-element.8.grad_in, f32[512,256]{1,0:T(8,128)S(1)} %get-tuple-element.9.hess_in), custom_call_target="tpu_custom_call" | custom-call | tf_op jit(solution)/shard_map/pallas_call | solution.py:638

commit v5 on v4

--- a/solution.py
+++ b/solution.py
@@ -183,15 +183,6 @@
     pull_halo_edge = functools.partial(half_copies, pulled, 0, ROWS - NEAR, NEAR, 10)
     last_halo = functools.partial(half_copies, pulled_2, 0, ROWS - NEAR, NEAR, 14)
 
-    pl.semaphore_wait(barrier, len(greeted))
-
-    coef_copies = neighbour_copies(
-        lambda start, count: raw.at[:, :, pl.ds(start, count), :], 0, ROWS - WIDE, WIDE, 0
-    )
-    start_all(coef_copies)
-    each_half(lambda q: start_all(ctrl_halo(q)))
-    tell()
-
     def shifted(pair):
         lanes = lax.broadcasted_iota(jnp.int32, pair[0].shape, 1)
         right = [pltpu.roll(x, LANES - 1, 1) for x in pair]
@@ -309,7 +300,7 @@
 
     def to_members(out, first):
         copies = []
-        for k in range(1, MEM_COUNT):
+        for k in (1, 7, 2, 6, 3, 5, 4):
             copies.append(
                 pltpu.make_async_remote_copy(
                     src_ref=out.at[m],
@@ -393,6 +384,15 @@
 
     four_sweeps(field, result, FORWARD, inner)
     project(mid_rows, mid_1)
+
+    pl.semaphore_wait(barrier, len(greeted))
+
+    coef_copies = neighbour_copies(
+        lambda start, count: raw.at[:, :, pl.ds(start, count), :], 0, ROWS - WIDE, WIDE, 0
+    )
+    start_all(coef_copies)
+    each_half(lambda q: start_all(ctrl_halo(q)))
+    tell()
     sent_m1 = to_members(mid_1, 1)
     hear()
     tell()

time: 46.5 us -> 46.4 us (level)
  no operation moved by 1% of the time
where the time goes in v5:
time: 46.4 us; the launch traced here: 46.3 us
  Pallas kernels  43.8 us (94%)
  between operations  2.41 us (5%)
    pallas_call x1, Pallas kernels, shards(): pl.pallas_call(kernel, out_shape=(jax.ShapeDtypeStruct((cells, width), f3...  42.9 us
    pallas_call x1, Pallas kernels, shards(): pl.pallas_call(hand_over, out_shape=(jax.ShapeDtypeStruct((cells, width),...  0.99 us

profile of v5, /device:TPU:1, one launch (start us, length us, event | category | flops | bytes accessed | tf_op | source)
XLA Modules:
  0.0 46.3 jit_solution(5388600767458272730)
XLA Ops:
  0.6 42.9 %shard_map.94 = (f32[512,256]{1,0:T(8,128)S(1)}, f32[512,256]{1,0:T(8,128)S(1)}, f32[1,1]{1,0:T(1,128)}) custom-call(f32[512,256]{1,0:T(8,128)} %bitcast.8, bf16[1536,256]{1,0:T(8,128)(2,1)} %bitcast.7, f32[48,256]{1,0:T(8,128)} %bitcast.9, f32[48,256]{1,0:T(8,128)} %bitcast.10, f32[16,256]{1,0:T(8,128)} %diff.1, f32[16,256]{1,0:T(8,128)} %adv.1, s32[16,256]{1,0:T(8,128)} %upw.1), custom_call_target="tpu_custom_call" | custom-call | tf_op jit(solution)/shard_map/pallas_call | solution.py:588
  43.5 1.0 %shard_map.95 = (f32[512,256]{1,0:T(8,128)}, f32[512,256]{1,0:T(8,128)}) custom-call(f32[512,256]{1,0:T(8,128)S(1)} %get-tuple-element.8.grad_in, f32[512,256]{1,0:T(8,128)S(1)} %get-tuple-element.9.hess_in), custom_call_target="tpu_custom_call" | custom-call | tf_op jit(solution)/shard_map/pallas_call | solution.py:638

commit v6 on v5

--- a/solution.py
+++ b/solution.py
@@ -529,6 +529,10 @@
     four_sweeps(pulled_2, result, ADJOINT, inner, add=grad)
     place(result, hess_nat, mid_rows)
 
+    for copies in (sent_e1, sent_m1, sent_e2, sent_m2):
+        for copy in copies:
+            copy.wait_send()
+
     def hessian_rim(q):
         wait_all(last_halo(q))
         four_sweeps(pulled_2, result, ADJOINT, near_rim, add=grad, half=q)
@@ -537,6 +541,8 @@
     place(result, hess_nat, edge_rows)
     store(hess_nat, hess_out, HALVES)
 
+    for copy in stores:
+        copy.wait()
     others = scal.at[pl.ds(0, TILE_COUNT - 1)]
     pltpu.make_async_remote_copy(
         src_ref=others,
@@ -552,12 +558,6 @@
     all_squares = jnp.sum(jnp.where(low_lane, sums[0], 0.0), axis=1, keepdims=True)
     all_observed = jnp.sum(jnp.where(low_lane, 0.0, sums[0]), axis=1, keepdims=True)
     step_out[...] = all_squares / (all_squares + all_observed)
-
-    for copies in (sent_e1, sent_m1, sent_e2, sent_m2):
-        for copy in copies:
-            copy.wait_send()
-    for copy in stores:
-        copy.wait()
 
 
 def hand_over(grad_in, hess_in, grad_out, hess_out, sem):

time: 46.4 us -> 46.3 us (level)
  no operation moved by 1% of the time
where the time goes in v6:
time: 46.3 us; the launch traced here: 46.2 us
  Pallas kernels  43.8 us (95%)
  between operations  2.41 us (5%)
    pallas_call x1, Pallas kernels, shards(): pl.pallas_call(kernel, out_shape=(jax.ShapeDtypeStruct((cells, width), f3...  42.8 us
    pallas_call x1, Pallas kernels, shards(): pl.pallas_call(hand_over, out_shape=(jax.ShapeDtypeStruct((cells, width),...  0.99 us

profile of v6, /device:TPU:1, one launch (start us, length us, event | category | flops | bytes accessed | tf_op | source)
XLA Modules:
  0.0 46.2 jit_solution(17460900237993302581)
XLA Ops:
  0.6 42.8 %shard_map.94 = (f32[512,256]{1,0:T(8,128)S(1)}, f32[512,256]{1,0:T(8,128)S(1)}, f32[1,1]{1,0:T(1,128)}) custom-call(f32[512,256]{1,0:T(8,128)} %bitcast.8, bf16[1536,256]{1,0:T(8,128)(2,1)} %bitcast.7, f32[48,256]{1,0:T(8,128)} %bitcast.9, f32[48,256]{1,0:T(8,128)} %bitcast.10, f32[16,256]{1,0:T(8,128)} %diff.1, f32[16,256]{1,0:T(8,128)} %adv.1, s32[16,256]{1,0:T(8,128)} %upw.1), custom_call_target="tpu_custom_call" | custom-call | tf_op jit(solution)/shard_map/pallas_call | solution.py:588
  43.5 1.0 %shard_map.95 = (f32[512,256]{1,0:T(8,128)}, f32[512,256]{1,0:T(8,128)}) custom-call(f32[512,256]{1,0:T(8,128)S(1)} %get-tuple-element.8.grad_in, f32[512,256]{1,0:T(8,128)S(1)} %get-tuple-element.9.hess_in), custom_call_target="tpu_custom_call" | custom-call | tf_op jit(solution)/shard_map/pallas_call | solution.py:638
